TPU v7x, 128 devices: a whole 4x4x4 slice. The times are simulated.
128 devices in a mesh: wake: 16 (over y_hi, x, core), grid: 8 (over z, y_lo).
Axes of the slice: x: 4, y: 4 (y_hi: 2, y_lo: 2; y = y_hi * 2 + y_lo), z: 4, core: 2. Of those that a mesh axis runs over, the one named last changes fastest.
Arguments:
- flow: float32 [5, 256, 131072], P(None, 'wake', 'grid'), may hold values from -6 to 6
- section_map: int32 [256, 131072], P('wake', 'grid'), may hold values from 0 to 2
- viscosity: float32 [3, 5], replicated, may hold values from 0.12 to 0.24
- particle_position: float32 [3, 32768], P(None, ('wake', 'grid')), may hold values from 0 to 1
- particle_strength: float32 [3, 32768], P(None, ('wake', 'grid')), may hold values from -0.6 to 0.6
- particle_core: float32 [32768], P(('wake', 'grid')), may hold values from 0.08 to 0.16
- shed_counts: int32 [16], replicated, may hold values from 512 to 2048, as said below
- node_position: float32 [3, 131072], P(None, ('wake', 'grid')), may hold values from 0 to 1
- node_block: int32 [131072, 1], P(('wake', 'grid')), may hold values from 0 to 15; in each aligned block of 1024 rows (0 to 1023, 1024 to 2047, ...) at most 128 rows name the same one
Outputs:
- flow_out: float32 [5, 256, 131072], P(None, 'wake', 'grid')
- particle_velocity: float32 [3, 32768], P(None, ('wake', 'grid'))
- particle_stretching: float32 [3, 32768], P(None, ('wake', 'grid'))
Inputs may be any that keep to these rules, and one draw needn't show every extreme that they name: `shed_counts`: at least one block holds 2048 live particles. `node_block`: among the 1024 nodes of one device (aligned blocks of nodes), at most 128 name any one block, and some block is named by exactly 128.
All inputs are finite; a program needn't handle non-finite values.
Results may differ from a plain program's by a relative error of at most 0.0003.
Values sent between devices are 32-bit elements; how exact they have to be, the bound alone decides.
A program may use at most 192 MiB of HBM per device.

v0:
```python
import math

import jax
import jax.numpy as jnp
from jax import lax
from jax.sharding import PartitionSpec as P

NSEC = 3
NODE_Z = 64
PB = 2048
SWEEPS = 3


inverse_four_pi = 1.0 / (4.0 * math.pi)


def from_behind(value, axis, by):
    count = lax.axis_size(axis)
    return lax.ppermute(value, axis, [(i, (i + by) % count) for i in range(count)])


def extended(cells, sides, width):
    for axis, dim in sides:
        count = lax.axis_size(axis)
        ends = count - 1
        head = lax.slice_in_dim(cells, 0, width, axis=dim)
        tail = lax.slice_in_dim(cells, cells.shape[dim] - width, cells.shape[dim], axis=dim)
        cells = jnp.concatenate(
            [
                lax.ppermute(tail, axis, [(i, (i + 1) % count) for i in range(ends)]),
                cells,
                lax.ppermute(head, axis, [((i + 1) % count, i) for i in range(ends)]),
            ],
            axis=dim,
        )
    return cells


def cross_three(first, second):
    return (
        first[1] * second[2] - first[2] * second[1],
        first[2] * second[0] - first[0] * second[2],
        first[0] * second[1] - first[1] * second[0],
    )


def particle_rates(place, spin, core, live, source, source_live):
    delta = [place[component][:, None] - source[component][None, :] for component in range(3)]
    spread = 0.5 * (core[:, None] * core[:, None] + source[6][None, :] * source[6][None, :])
    distance = delta[0] * delta[0] + delta[1] * delta[1] + delta[2] * delta[2] + spread
    weight = jnp.where(source_live[None, :], distance ** (-1.5), 0.0)
    steep = 3.0 * weight / distance
    source_spin = [source[3 + component][None, :] for component in range(3)]
    curl = cross_three(delta, source_spin)
    along = spin[0][:, None] * delta[0] + spin[1][:, None] * delta[1] + spin[2][:, None] * delta[2]
    velocity = jnp.stack([jnp.sum(weight * curl[component], axis=1) for component in range(3)])
    spin_sum = [jnp.sum(weight * source_spin[component], axis=1) for component in range(3)]
    bent = jnp.stack([jnp.sum(steep * along * curl[component], axis=1) for component in range(3)])
    turned = jnp.stack(cross_three(spin, spin_sum))
    factor = jnp.where(live, -inverse_four_pi, 0.0)[None, :]
    return (velocity * factor, (turned - bent) * factor)


def node_rates(points, source, source_live):
    delta = [points[component][:, None] - source[component][None, :] for component in range(3)]
    distance = (
        delta[0] * delta[0]
        + delta[1] * delta[1]
        + delta[2] * delta[2]
        + source[6][None, :] * source[6][None, :]
    )
    weight = jnp.where(source_live[None, :], distance ** (-1.5), 0.0)
    source_spin = [source[3 + component][None, :] for component in range(3)]
    curl = cross_three(delta, source_spin)
    return (
        jnp.stack([jnp.sum(weight * curl[component], axis=1) for component in range(3)])
        * -inverse_four_pi
    )


def tiled(function, arrays, count):
    tile = math.gcd(count, 256)
    pieces = count // tile

    def split_tiles(array):
        return jnp.moveaxis(array.reshape(array.shape[:-1] + (pieces, tile)), -2, 0)

    def join_tiles(array):
        moved = jnp.moveaxis(array, 0, -2)
        return moved.reshape(moved.shape[:-2] + (count,))

    results = lax.map(function, tuple((split_tiles(array) for array in arrays)))
    return jax.tree.map(join_tiles, results)


def cell_diffusion(sections, viscosity):
    total = jnp.zeros((5,) + sections.shape, jnp.float32)
    for number in range(NSEC):
        total = total + jnp.where(sections[None] == number, viscosity[number][:, None, None], 0.0)
    return total


def on_device(
    flow,
    section_map,
    viscosity,
    particle_position,
    particle_strength,
    particle_core,
    shed_counts,
    node_position,
    node_block,
):
    wake_count = lax.axis_size("wake")
    wake_index = lax.axis_index("wake")
    stops = wake_count // 2
    half = stops // 2
    slots = jnp.arange(PB, dtype=jnp.int32)
    target_count = particle_position.shape[1]
    target_slots = lax.axis_index("grid") * target_count + jnp.arange(target_count, dtype=jnp.int32)
    target_live = target_slots < shed_counts[wake_index]
    share = jnp.concatenate([particle_position, particle_strength, particle_core[None, :]], axis=0)
    block = lax.all_gather(share, "grid", axis=1, tiled=True)

    def visit(source, number, totals):
        source_live = slots < shed_counts[number]

        def visit_rates(arrays):
            return particle_rates(arrays[0], arrays[1], arrays[2], arrays[3], source, source_live)

        velocity, stretch = tiled(
            visit_rates,
            (particle_position, particle_strength, particle_core, target_live),
            target_count,
        )
        return (totals[0] + velocity, totals[1] + stretch)

    zeros = jnp.zeros((3, target_count), jnp.float32)
    first = from_behind(block, "wake", 1 - half)
    totals = visit(first, (wake_index + half - 1) % wake_count, (zeros, zeros))

    def advance(turn, carry):
        source, sums = carry
        source = from_behind(source, "wake", 1)
        return (source, visit(source, (wake_index + half - 1 - turn) % wake_count, sums))

    carried, totals = lax.fori_loop(1, stops, advance, (first, totals))
    node_count = node_position.shape[1]
    target_block = node_block[:, 0]
    capacity = 2 * node_count // wake_count
    onehot = (target_block[:, None] == jnp.arange(wake_count, dtype=jnp.int32)[None, :]).astype(
        jnp.int32
    )
    rank = jnp.sum((jnp.cumsum(onehot, axis=0) - onehot) * onehot, axis=1)
    slot = target_block * capacity + rank
    outgoing = jnp.zeros((3, wake_count * capacity), jnp.float32).at[:, slot].set(node_position)
    outgoing = outgoing.reshape(3, wake_count, capacity)
    own_live = slots < shed_counts[wake_index]
    points = lax.all_to_all(outgoing, "wake", split_axis=1, concat_axis=1, tiled=True)
    flat = points.reshape(3, -1)

    def evaluate_rates(arrays):
        return node_rates(arrays[0], block, own_live)

    result = tiled(evaluate_rates, (flat,), flat.shape[1])
    answered = result.reshape(points.shape)
    returned = lax.all_to_all(answered, "wake", split_axis=1, concat_axis=1, tiled=True)
    node_velocity = returned.reshape(3, wake_count * capacity)[:, slot]
    rows = flow.shape[1]
    columns = flow.shape[2]
    stride = columns // NODE_Z
    field = flow.at[1:4, :, ::stride].set(node_velocity.reshape(3, rows, NODE_Z))
    diffusion = cell_diffusion(section_map, viscosity)
    for sweep in range(SWEEPS):
        padded = extended(field, (("wake", 1), ("grid", 2)), 1)
        beside = (
            padded[:, 2:, 1:-1] + padded[:, :-2, 1:-1] + padded[:, 1:-1, 2:] + padded[:, 1:-1, :-2]
        )
        field = field + diffusion * (beside - 4.0 * field)
    return (field, totals[0], totals[1])


def solution(mesh):
    return jax.shard_map(
        on_device,
        mesh=mesh,
        in_specs=(
            P(None, "wake", "grid"),
            P("wake", "grid"),
            P(),
            P(None, ("wake", "grid")),
            P(None, ("wake", "grid")),
            P(("wake", "grid")),
            P(),
            P(None, ("wake", "grid")),
            P(("wake", "grid"), None),
        ),
        out_specs=(P(None, "wake", "grid"), P(None, ("wake", "grid")), P(None, ("wake", "grid"))),
        check_vma=False,
    )
```

profile of v0, /device:TPU:39, one launch (start us, length us, event | category | flops | bytes accessed | tf_op | source)
XLA Modules:
  0.0 856.5 jit_solution(195151444402644081)
XLA Ops:
  1.5 4.5 reduce-window.6
  8.8 3.3 scatter_custom_fusion
  13.0 7.7 all-to-all-start
  20.8 22.6 %all_gather.3 = f32[7,2048]{1,0:T(8,128)} all-gather(f32[7,256]{1,0:T(8,128)S(1)} %pad_maximum_fusion.33), channel_id=1, replica_groups=mesh['wake'=16,'grid'=8] {'grid'}, dimensions={1}, use_global_device_ids=true | all-gather | bytes 64512 | tf_op jit(solution)/shard_map/all_gather | solution.py:123
  43.4 7.2 collective-permute-start.13
  52.6 42.7 %while.50 = (s32[]{:T(128)}, f32[8,3,256]{2,1,0:T(4,128)}, f32[8,3,256]{2,0,1:T(8,128)S(1)}, f32[7,2048]{1,0:T(8,128)}, f32[1,2048]{1,0:T(1,128)S(1)}, /*index=5*/s32[]{:T(128)}, s32[]{:T(128)}, s32[]{:T(128)}, s32[]{}, s32[]{}) while((s32[]{:T(128)}, f32[8,3,256]{2,1,0:T(4,128)}, f32[8,3,256]{2,0,1:T(8,128)S(1)}, ...), condition=%wide.region_8.9_spmd.clone, body=%wide.region_4.8_spmd.clone.sunk | while | flops 13110788 | bytes 179853 | solution.py:92
  54.4 2.9 fusion.113
  59.7 2.9 fusion.113
  65.1 2.9 fusion.113
  70.4 2.9 fusion.113
  75.7 2.9 fusion.113
  81.1 2.9 fusion.113
  86.4 2.9 fusion.113
  91.7 2.9 fusion.113
  95.3 6.7 all-to-all-start.1
  102.0 20.3 %copy.69 = f32[5,16,16384]{1,2,0:T(8,128)} copy(f32[5,16,16384]{2,1,0:T(8,128)} %param.13) | data formatting | bytes 10485760
  122.7 2.8 gather_fusion
  126.0 489.6 %while.49 = (s32[]{:T(128)}, f32[5,16,16384]{1,2,0:T(8,128)}, s32[64,2]{0,1:T(2,128)S(1)}, f32[64,3,16]{2,0,1:T(8,128)S(1)}, s32[]{:T(128)}, /*index=5*/s32[3]{0:T(128)S(1)}, s32[1]{0:T(128)}, s32[]{:T(128)}) while((s32[]{:T(128)}, f32[5,16,16384]{1,2,0:T(8,128)}, s32[64,2]{0,1:T(2,128)S(1)}, f32[64,3,16]{2,0,1:T(8,128)S(1)}, s32[]{:T(128)}, ...), condition=%wide.while_cond, body=%wide.while_body.sunk | while | flops 67 | bytes 1123 | solution.py:172
  128.6 2.6 broadcast_select_fusion.2
  136.3 2.6 broadcast_select_fusion.2
  159.2 2.6 broadcast_select_fusion.2
  174.5 2.6 broadcast_select_fusion.2
  258.6 2.6 broadcast_select_fusion.2
  266.3 2.6 broadcast_select_fusion.2
  304.5 2.6 broadcast_select_fusion.2
  312.2 2.6 broadcast_select_fusion.2
  319.8 2.6 broadcast_select_fusion.2
  342.8 2.6 broadcast_select_fusion.2
  381.0 2.6 broadcast_select_fusion.2
  472.8 2.6 broadcast_select_fusion.2
  480.5 2.6 broadcast_select_fusion.2
  557.0 2.6 broadcast_select_fusion.2
  572.3 2.6 broadcast_select_fusion.2
  615.6 27.6 %copy.76 = f32[5,16,16384]{2,0,1:T(8,128)} copy(f32[5,16,16384]{1,2,0:T(8,128)} %get-tuple-element.407) | data formatting | bytes 10485760 | tf_op jit(solution)/shard_map/scatter | solution.py:172
  646.8 6.9 collective-permute-start.2
  654.3 4.3 collective-permute-done.1
  660.8 4.4 collective-permute-start.3
  667.2 4.1 collective-permute-done.4
  671.3 17.5 %fusion.60 = f32[5,16,16384]{2,0,1:T(8,128)S(1)} fusion(f32[5,16,16384]{2,0,1:T(8,128)} %copy.76, f32[5,18,1]{2,0,1:T(8,128)S(1)} %collective-permute-done.4, f32[5,1,16384]{2,0,1:T(8,128)S(1)} %collective-permute-done.1, f32[5,1,16384]{2,0,1:T(8,128)S(1)} %collective-permute-done.2, f32[5,18,1]{2,0,1:T(8,128)S(1)} %collective-permute-done.3, ...), kind=kLoop, calls=%fused_computation.117 | loop fusion | flops 26214400 | bytes 11928332 | tf_op jit(solution)/shard_map/add | solution.py:179
  690.8 10.1 %collective-permute-start.6 = (f32[5,1,16384]{2,0,1:T(8,128)S(1)}, f32[5,1,16384]{2,0,1:T(8,128)S(1)}, u32[]{:S(2)}, u32[]{:S(2)}) collective-permute-start(f32[5,1,16384]{2,0,1:T(8,128)S(1)} %get-tuple-element.603), channel_id=1, source_target_pairs={{0,8},{8,16},{16,24},{24,32},{32,40},{40,48},{48,56},{56,64},{64,7... | collective-permute-start | bytes 983048 | tf_op jit(solution)/shard_map/ppermute | solution.py:30
  701.5 4.4 collective-permute-done.5
  709.0 3.5 collective-permute-start.8
  715.0 11.0 %fusion.54 = f32[5,16,16384]{2,0,1:T(8,128)S(1)} fusion(f32[5,16,16384]{2,0,1:T(8,128)S(1)} %fusion.60, f32[5,18,1]{2,0,1:T(8,128)S(1)} %collective-permute-done.8, f32[5,1,16384]{2,0,1:T(8,128)S(1)} %collective-permute-done.5, f32[5,1,16384]{2,0,1:T(8,128)S(1)} %collective-permute-done.6, f32[5,18,1]{2,0,1:T(8,128)S(1)} %collective-permute-done.7, ...), kind=kLoop, calls=%fused_computation.103 | loop fusion | flops 26214400 | bytes 11928332 | tf_op jit(solution)/shard_map/add | solution.py:179
  726.1 9.2 %collective-permute-start.10 = (f32[5,1,16384]{2,0,1:T(8,128)S(1)}, f32[5,1,16384]{2,0,1:T(8,128)S(1)}, u32[]{:S(2)}, u32[]{:S(2)}) collective-permute-start(f32[5,1,16384]{2,0,1:T(8,128)S(1)} %get-tuple-element.601), channel_id=1, source_target_pairs={{0,8},{8,16},{16,24},{24,32},{32,40},{40,48},{48,56},{56,64},{64,7... | collective-permute-start | bytes 983048 | tf_op jit(solution)/shard_map/ppermute | solution.py:30
  737.2 5.0 fusion.79
  742.3 7.3 collective-permute-done.9
  751.5 3.4 collective-permute-start.12
  755.0 2.6 collective-permute-done.12
  757.5 11.0 %fusion.48 = f32[5,16,16384]{2,0,1:T(8,128)S(1)} fusion(f32[5,16,16384]{2,0,1:T(8,128)S(1)} %fusion.54, f32[5,18,1]{2,0,1:T(8,128)S(1)} %collective-permute-done.12, f32[5,1,16384]{2,0,1:T(8,128)S(1)} %collective-permute-done.9, f32[5,1,16384]{2,0,1:T(8,128)S(1)} %collective-permute-done.10, f32[5,18,1]{2,0,1:T(8,128)S(1)} %collective-permute-done.11, ...), kind=kLoop, calls=%fused_computation.89 | loop fusion | flops 26214400 | bytes 11928332 | tf_op jit(solution)/shard_map/add | solution.py:179
  768.6 5.4 copy.77
  773.9 82.0 %while.51 = (s32[]{:T(128)}, f32[7,2048]{1,0:T(8,128)S(1)}, f32[3,256]{1,0:T(4,128)S(1)}, f32[3,256]{1,0:T(4,128)S(1)}, s32[]{:T(128)}, /*index=5*/s32[16]{0:T(1...) while((s32[]{:T(128)}, f32[7,2048]{1,0:T(8,128)S(1)}, ...), condition=%wide.region_29.30_spmd.clone, body=%wide.region_19.29_spmd.clone.sunk | while | flops 24654864 | bytes 581992 | solution.py:147
  776.7 4.9 fusion.117
  781.7 5.6 collective-permute-start
  789.1 4.9 fusion.117
  794.1 5.6 collective-permute-start
  801.5 4.9 fusion.117
  806.4 5.6 collective-permute-start
  813.9 4.9 fusion.117
  818.8 5.6 collective-permute-start
  826.2 4.9 fusion.117
  831.2 5.6 collective-permute-start
  838.6 4.9 fusion.117
  843.5 5.6 collective-permute-start
  851.0 4.9 fusion.117
  (473 shorter events, 512.0 us)
Async XLA Ops:
  0.6 20.1 %copy-start.6 = (f32[256]{0:T(256)S(1)}, f32[256]{0:T(256)}, u32[]{:S(2)}) copy-start(f32[256]{0:T(256)} %param.18) | copy-start | bytes 3076
  0.6 20.1 %copy-start.4 = (f32[3,256]{1,0:T(4,128)S(1)}, f32[3,256]{1,0:T(4,128)}, u32[]{:S(2)}) copy-start(f32[3,256]{1,0:T(4,128)} %param.16) | copy-start | bytes 9220
  0.7 20.1 %copy-start.1 = (f32[3,256]{1,0:T(4,128)S(1)}, f32[3,256]{1,0:T(4,128)}, u32[]{:S(2)}) copy-start(f32[3,256]{1,0:T(4,128)} %param.17) | copy-start | bytes 9220
  0.7 50.8 %copy-start = (s32[16,16384]{1,0:T(8,128)S(1)}, s32[16,16384]{1,0:T(8,128)}, u32[]{:S(2)}) copy-start(s32[16,16384]{1,0:T(8,128)} %param.14) | copy-start | bytes 3145732
  8.7 43.2 %copy-start.8 = (f32[3,5]{1,0:T(4,128)S(1)}, f32[3,5]{1,0:T(4,128)}, u32[]{:S(2)}) copy-start(f32[3,5]{1,0:T(4,128)} %param.15) | copy-start | bytes 184
  8.7 43.2 %copy-start.7 = (s32[16]{0:T(128)S(1)}, s32[16]{0:T(128)}, u32[]{:S(2)}) copy-start(s32[16]{0:T(128)} %param.19) | copy-start | bytes 196
  13.0 39.5 %all-to-all-start = ((f32[3,16,128]{2,0,1:T(4,128)}), f32[3,16,128]{2,0,1:T(4,128)S(1)}, u32[]{:S(2)}, u32[]{:S(2)}) async-start(f32[3,16,128]{2,0,1:T(4,128)} %copy.62), calls=%async_computation | async-start | bytes 65536 | tf_op jit(solution)/shard_map/all_to_all | solution.py:159
  43.4 669.2 %collective-permute-start.13 = (f32[7,2048]{1,0:T(8,128)}, f32[7,2048]{1,0:T(8,128)S(1)}, u32[]{:S(2)}, u32[]{:S(2)}) collective-permute-start(f32[7,2048]{1,0:T(8,128)} %all_gather.3), channel_id=1, source_target_pairs={{0,104},{8,112},{16,120},{24,0},{32,8},{40,16},{48,24},{56,32},{64... | collective-permute-start | bytes 172040 | tf_op jit(solution)/shard_map/ppermute | solution.py:19
  95.3 27.0 %all-to-all-start.1 = ((f32[3,16,128]{2,0,1:T(4,128)}), f32[3,16,128]{2,0,1:T(4,128)S(1)}, u32[]{:S(2)}, u32[]{:S(2)}) async-start(f32[3,16,128]{2,0,1:T(4,128)} %bitcast.12), calls=%async_computation.1 | async-start | bytes 65536 | tf_op jit(solution)/shard_map/all_to_all | solution.py:167
  102.0 24.0 %copy-start.5 = (s32[3]{0:T(128)S(1)}, s32[3]{0:T(128)}, u32[]{:S(2)}) copy-start(s32[3]{0:T(128)} %constant.451) | copy-start | bytes 40
  644.5 14.1 %collective-permute-start.1 = (f32[5,1,16384]{2,0,1:T(8,128)S(1)}, f32[5,1,16384]{2,0,1:T(8,128)S(1)}, u32[]{:S(2)}, u32[]{:S(2)}) collective-permute-start(f32[5,1,16384]{2,0,1:T(8,128)S(1)} %get-tuple-element.606), channel_id=1, source_target_pairs={{8,0},{16,8},{24,16},{32,24},{40,32},{48,40},{56,48},{64,56},{72,6... | collective-permute-start | bytes 983048 | tf_op jit(solution)/shard_map/ppermute | solution.py:32
  646.8 13.1 %collective-permute-start.2 = (f32[5,1,16384]{2,0,1:T(8,128)S(1)}, f32[5,1,16384]{2,0,1:T(8,128)S(1)}, u32[]{:S(2)}, u32[]{:S(2)}) collective-permute-start(f32[5,1,16384]{2,0,1:T(8,128)S(1)} %get-tuple-element.605), channel_id=1, source_target_pairs={{0,8},{8,16},{16,24},{24,32},{32,40},{40,48},{48,56},{56,64},{64,7... | collective-permute-start | bytes 983048 | tf_op jit(solution)/shard_map/ppermute | solution.py:30
  660.8 6.4 collective-permute-start.3
  665.3 6.0 collective-permute-start.4
  688.8 17.1 %collective-permute-start.5 = (f32[5,1,16384]{2,0,1:T(8,128)S(1)}, f32[5,1,16384]{2,0,1:T(8,128)S(1)}, u32[]{:S(2)}, u32[]{:S(2)}) collective-permute-start(f32[5,1,16384]{2,0,1:T(8,128)S(1)} %get-tuple-element.604), channel_id=1, source_target_pairs={{8,0},{16,8},{24,16},{32,24},{40,32},{48,40},{56,48},{64,56},{72,6... | collective-permute-start | bytes 983048 | tf_op jit(solution)/shard_map/ppermute | solution.py:32
  690.8 16.2 %collective-permute-start.6 = (f32[5,1,16384]{2,0,1:T(8,128)S(1)}, f32[5,1,16384]{2,0,1:T(8,128)S(1)}, u32[]{:S(2)}, u32[]{:S(2)}) collective-permute-start(f32[5,1,16384]{2,0,1:T(8,128)S(1)} %get-tuple-element.603), channel_id=1, source_target_pairs={{0,8},{8,16},{16,24},{24,32},{32,40},{40,48},{48,56},{56,64},{64,7... | collective-permute-start | bytes 983048 | tf_op jit(solution)/shard_map/ppermute | solution.py:30
  707.1 5.5 collective-permute-start.7
  709.0 6.0 collective-permute-start.8
  726.1 16.2 %collective-permute-start.10 = (f32[5,1,16384]{2,0,1:T(8,128)S(1)}, f32[5,1,16384]{2,0,1:T(8,128)S(1)}, u32[]{:S(2)}, u32[]{:S(2)}) collective-permute-start(f32[5,1,16384]{2,0,1:T(8,128)S(1)} %get-tuple-element.601), channel_id=1, source_target_pairs={{0,8},{8,16},{16,24},{24,32},{32,40},{40,48},{48,56},{56,64},{64,7... | collective-permute-start | bytes 983048 | tf_op jit(solution)/shard_map/ppermute | solution.py:30
  735.3 14.2 %collective-permute-start.9 = (f32[5,1,16384]{2,0,1:T(8,128)S(1)}, f32[5,1,16384]{2,0,1:T(8,128)S(1)}, u32[]{:S(2)}, u32[]{:S(2)}) collective-permute-start(f32[5,1,16384]{2,0,1:T(8,128)S(1)} %get-tuple-element.602), channel_id=1, source_target_pairs={{8,0},{16,8},{24,16},{32,24},{40,32},{48,40},{56,48},{64,56},{72,6... | collective-permute-start | bytes 983048 | tf_op jit(solution)/shard_map/ppermute | solution.py:32
  749.6 5.3 collective-permute-start.11
  751.5 6.0 collective-permute-start.12
  773.9 2.7 collective-permute-start
  781.7 7.4 collective-permute-start
  794.1 7.4 collective-permute-start
  806.4 7.4 collective-permute-start
  818.8 7.4 collective-permute-start
  831.2 7.4 collective-permute-start
  843.5 7.4 collective-permute-start
  855.9 0.6 copy-start.2
  855.9 0.6 copy-start.3
where the time goes:
time: 872 us; the launch traced here: 857 us
  other arithmetic  422 us (48%)
  local copies, waits for them, and re-layouts  277 us (32%)
  starting transfers between devices  105 us (12%)
  waiting for transfers between devices  27.4 us (3%)
  blocking collectives  22.6 us (3%)
    scatter x128, other arithmetic  291 us
    scatter x192, local copies, waits for them, and re-layouts  198 us
    ppermute x8, starting transfers between devices, from_behind(): lax.ppermute(value, axis, [(i, (i + by) % count) for i in range(count)])  41.4 us
    add x3, other arithmetic, on_device(): field = field + diffusion * (beside - 4.0 * field)  39.5 us
    reduce_sum x8, other arithmetic, particle_rates(): jnp.sum(steep * along * curl[component], axis=1)  39.1 us
    ppermute x6, starting transfers between devices, extended(): lax.ppermute(tail, axis, [(i, (i + 1) % count) for i in range(ends)])  35.1 us
    scatter x1, local copies, waits for them, and re-layouts, on_device(): flow.at[1:4, :, ::stride].set(node_velocity.reshape(3, rows, NODE_Z))  27.6 us
    unnamed x21, local copies, waits for them, and re-layouts  27.3 us
  transfers between devices with their start and end apart: 22, of which 8 were waited for; matrix products, arithmetic and copies ran while one was open for 73% of the time, Pallas kernels for 0%

commit v1 on v0

v1 whole, which is shorter than its diff:
```python
import math

import jax
import jax.numpy as jnp
from jax import lax
from jax.experimental import pallas as pl
from jax.experimental.pallas import tpu as pltpu
from jax.sharding import PartitionSpec as P

PB = 2048
NW = 16
NG = 8
CHUNK = 512
UNROLL = 4
PAIRED = 2
TILE = 64
SWEEPS = 3
BF = jnp.bfloat16
F32 = jnp.float32
MESH = pl.DeviceIdType.MESH
SCALE = -1.0 / (4.0 * math.pi)
WHOLE = pl.BlockSpec(memory_space=pltpu.VMEM)


def split_three(value):
    high = value.astype(BF).astype(F32)
    rest = value - high
    middle = rest.astype(BF).astype(F32)
    return high, middle, rest - middle


def dot_nt(first, second):
    return lax.dot_general(first, second, (((1,), (1,)), ((), ())), preferred_element_type=F32)


def cross_rows(first, second):
    return [
        first[1] * second[2] - first[2] * second[1],
        first[2] * second[0] - first[0] * second[2],
        first[0] * second[1] - first[1] * second[0],
    ]


def target_rows(place, weight, halved):
    ones = jnp.ones_like(weight)
    none = jnp.zeros_like(weight)
    parts = split_three(jnp.concatenate([-2.0 * row for row in place] + [none, none, weight, none, none], axis=0))
    unit = jnp.concatenate([none] * 3 + [none if halved else ones, ones if halved else none] + [none] * 3, axis=0)
    high, middle, low = parts
    return jnp.concatenate([high + unit, middle, low, high + unit, middle, high + unit], axis=0).astype(BF)


def source_rows(rows, live):
    place = rows[0:3]
    square = place[0] * place[0] + place[1] * place[1] + place[2] * place[2]
    core = rows[6] * rows[6]
    half = square + 0.5 * core
    ones = jnp.ones_like(square)
    none = jnp.zeros_like(square)
    high, middle, low = split_three(
        jnp.concatenate(list(place) + [square + core, half, ones, none, none], axis=0)
    )
    distance = jnp.concatenate([high, high, high, middle, middle, low], axis=0).astype(BF)
    spin = [jnp.where(live, rows[3 + c], 0.0) for c in range(3)]
    moment = jnp.concatenate(spin + cross_rows(place, spin) + [none, none], axis=0)
    return distance, moment, half


def gather_kernel(
    place, spin, core, node_place, node_block, gathered, points, slot_out, amounts,
    send_one, recv_one, send_two, recv_two, send_three, recv_three,
):
    wake = lax.axis_index("wake")
    grid = lax.axis_index("grid")
    side = lax.rem(wake, 2)
    pair = wake // 2
    sibling = wake + 1 - 2 * side
    lanes = pl.ds(pl.multiple_of(grid * 256, 256), 256)
    mine = gathered.at[pair, side, :, lanes]

    barrier = pltpu.get_barrier_semaphore()
    for turn in range(1, NG):
        pl.semaphore_signal(
            barrier, inc=1, device_id={"wake": wake, "grid": lax.rem(grid + turn, NG)}, device_id_type=MESH
        )
        pl.semaphore_signal(
            barrier, inc=1, device_id={"wake": lax.rem(wake + 2 * turn, NW), "grid": grid}, device_id_type=MESH
        )
    pl.semaphore_signal(barrier, inc=1, device_id={"wake": sibling, "grid": grid}, device_id_type=MESH)
    mine[...] = jnp.concatenate(
        [place[...], spin[...], core[...], jnp.zeros((1, 256), F32)], axis=0
    )
    pl.semaphore_wait(barrier, 2 * NG - 1)

    first = []
    for turn in range(1, NG):
        copy = pltpu.make_async_remote_copy(
            src_ref=mine,
            dst_ref=mine,
            send_sem=send_one.at[turn - 1],
            recv_sem=recv_one.at[turn - 1],
            device_id={"wake": wake, "grid": lax.rem(grid + turn, NG)},
            device_id_type=MESH,
        )
        copy.start()
        first.append(copy)

    names = node_block[...]
    spots = [node_place[c : c + 1, :] - 0.5 for c in range(3)]
    weight = spots[0] * spots[0] + spots[1] * spots[1] + spots[2] * spots[2]
    rows = target_rows(spots, weight, False)
    members = jnp.where(lax.broadcasted_iota(jnp.int32, (NW, 1024), 0) == names, 1.0, 0.0)
    triangle = jnp.where(
        lax.broadcasted_iota(jnp.int32, (128, 128), 0) <= lax.broadcasted_iota(jnp.int32, (128, 128), 1),
        1.0,
        0.0,
    ).astype(BF)
    pieces = jnp.concatenate([members[:, 128 * k : 128 * (k + 1)] for k in range(8)], axis=0)
    running = jnp.dot(pieces.astype(BF), triangle, preferred_element_type=F32)
    before = jnp.zeros((NW, 1), F32)
    ranks = []
    for k in range(8):
        part = running[NW * k : NW * (k + 1)]
        ranks.append(part + before)
        before = before + part[:, 127:128]
    rank = jnp.sum(members * jnp.concatenate(ranks, axis=1), axis=0, keepdims=True) - 1.0
    slot = names * 128 + rank.astype(jnp.int32)
    slot_out[...] = slot
    amounts[...] = jnp.broadcast_to(before, (NW, 128)).astype(jnp.int32)

    for copy in first:
        copy.wait_recv()
    second = []
    for turn in range(1, NG):
        copy = pltpu.make_async_remote_copy(
            src_ref=gathered.at[pair, side],
            dst_ref=gathered.at[pair, side],
            send_sem=send_two.at[turn - 1],
            recv_sem=recv_two.at[turn - 1],
            device_id={"wake": lax.rem(wake + 2 * turn, NW), "grid": grid},
            device_id_type=MESH,
        )
        copy.start()
        second.append(copy)

    def place_nodes(part, carry):
        start = pl.multiple_of(part * 256, 256)
        chosen = jnp.where(
            lax.broadcasted_iota(jnp.int32, (256, 1024), 0) + part * 256 == slot, 1.0, 0.0
        ).astype(BF)
        points[pl.ds(start, 256), :] = dot_nt(chosen, rows).astype(BF)
        return carry

    lax.fori_loop(0, 8, place_nodes, 0)

    for copy in second:
        copy.wait_recv()
    third = pltpu.make_async_remote_copy(
        src_ref=gathered.at[:, side],
        dst_ref=gathered.at[:, side],
        send_sem=send_three.at[0],
        recv_sem=recv_three.at[0],
        device_id={"wake": sibling, "grid": grid},
        device_id_type=MESH,
    )
    third.start()
    for copy in first + second:
        copy.wait_send()
    third.wait()


def gather_particles(place, spin, core, node_place, node_block):
    return pl.pallas_call(
        gather_kernel,
        out_shape=[
            jax.ShapeDtypeStruct((NW // 2, 2, 8, PB), F32),
            jax.ShapeDtypeStruct((NW * 128, 48), BF),
            jax.ShapeDtypeStruct((1, 1024), jnp.int32),
            jax.ShapeDtypeStruct((NW, 128), jnp.int32),
        ],
        in_specs=[WHOLE] * 5,
        out_specs=[WHOLE] * 4,
        scratch_shapes=[
            pltpu.SemaphoreType.DMA((NG - 1,)),
            pltpu.SemaphoreType.DMA((NG - 1,)),
            pltpu.SemaphoreType.DMA((NG - 1,)),
            pltpu.SemaphoreType.DMA((NG - 1,)),
            pltpu.SemaphoreType.DMA((1,)),
            pltpu.SemaphoreType.DMA((1,)),
        ],
        compiler_params=pltpu.CompilerParams(
            collective_id=0, has_side_effects=True, vmem_limit_bytes=32 << 20
        ),
        cost_estimate=pl.CostEstimate(flops=1 << 28, bytes_accessed=4 << 20, transcendentals=0),
    )(place, spin, core, node_place, node_block)


def build_source(counts, gathered, block, start, size):
    tile = gathered[block // 2, lax.rem(block, 2), :, pl.ds(start, size)]
    live = start + lax.broadcasted_iota(jnp.int32, (1, size), 1) < counts[block]
    source = [tile[c : c + 1] - 0.5 for c in range(3)] + [tile[c : c + 1] for c in range(3, 7)]
    distance, moment, half = source_rows(source, live)
    return distance, moment, source, half


def node_kernel(counts, amounts, gathered, points, slot, node_place, node_out, distance_rows, moment_rows, total):
    def build(block, carry):
        def step(chunk, inner):
            start = pl.multiple_of(chunk * CHUNK, CHUNK)
            distance, moment, _, _ = build_source(counts, gathered, block, start, CHUNK)
            high, middle, low = split_three(moment)
            distance_rows[block, :, pl.ds(start, CHUNK)] = distance
            moment_rows[block, :, pl.ds(start, CHUNK)] = jnp.concatenate(
                [high, middle, low, jnp.zeros_like(low)], axis=0
            ).astype(BF)
            return inner

        return lax.fori_loop(0, pl.cdiv(counts[block], CHUNK), step, carry)

    lax.fori_loop(0, NW, build, 0)
    total[...] = jnp.zeros_like(total)

    def count_items(block, amount):
        return amount + pl.cdiv(amounts[block, 0], TILE) * pl.cdiv(counts[block], CHUNK)

    items = lax.fori_loop(0, NW, count_items, 0)

    def advance(block, part, chunk):
        safe = jnp.minimum(block, NW - 1)
        parts = pl.cdiv(amounts[safe, 0], TILE)
        chunks = pl.cdiv(counts[safe], CHUNK)
        end = chunk + 1 >= chunks
        last = end & (part + 1 >= parts)
        return (
            jnp.where(last, block + 1, block),
            jnp.where(last, 0, jnp.where(end, part + 1, part)),
            jnp.where(end, 0, chunk + 1),
        )

    def skip(block):
        def empty(at):
            return (at < NW) & (amounts[jnp.minimum(at, NW - 1), 0] == 0)

        return lax.while_loop(empty, lambda at: at + 1, block)

    def run(turn, carry):
        block, part, chunk = carry
        added = []
        for _ in range(UNROLL):
            block = skip(block)
            safe = jnp.minimum(block, NW - 1)
            row = jnp.where(block < NW, safe * 2 + part, 2 * NW)
            start = pl.multiple_of(chunk * CHUNK, CHUNK)
            point = points[pl.ds(pl.multiple_of(jnp.minimum(row, 2 * NW - 1) * TILE, TILE), TILE), :]
            distance = distance_rows[safe, :, pl.ds(start, CHUNK)]
            columns = moment_rows[safe, :, pl.ds(start, CHUNK)]
            root = lax.rsqrt(jnp.dot(point, distance, preferred_element_type=F32))
            third = root * root * root
            high = third.astype(BF)
            low = (third - high.astype(F32)).astype(BF)
            gain = dot_nt(jnp.concatenate([high, low], axis=0), columns)
            added.append((row, gain[0:TILE] + gain[TILE : 2 * TILE]))
            block, part, chunk = advance(block, part, chunk)
        for row, gain in added:
            where = pl.ds(pl.multiple_of(row * TILE, TILE), TILE)
            total[where, :] += gain
        return block, part, chunk

    lax.fori_loop(0, pl.cdiv(items, UNROLL), run, (0, 0, 0))

    slots = jnp.transpose(jnp.broadcast_to(slot[...].astype(F32), (8, 1024)))[:, 0:1].astype(jnp.int32)
    found = jnp.zeros((1024, 32), F32)
    for block in range(NW):
        gained = total[128 * block : 128 * (block + 1), :]
        gained = gained[:, 0:8] + gained[:, 8:16] + gained[:, 16:24]
        used = lax.broadcasted_iota(jnp.int32, (128, 8), 0) < amounts[block, 0]
        high, middle, low = split_three(jnp.where(used, gained, 0.0))
        stacked = jnp.concatenate([high, middle, low, jnp.zeros_like(low)], axis=1).astype(BF)
        chosen = jnp.where(
            lax.broadcasted_iota(jnp.int32, (1024, 128), 1) + block * 128 == slots, 1.0, 0.0
        ).astype(BF)
        found = found + jnp.dot(chosen, stacked, preferred_element_type=F32)
    found = jnp.transpose(jnp.concatenate([found, jnp.zeros((1024, 96), F32)], axis=1))
    found = found[0:8] + found[8:16] + found[16:24]
    spots = [node_place[c : c + 1, :] - 0.5 for c in range(3)]
    moved = cross_rows(spots, [found[c : c + 1] for c in range(3)])
    for c in range(3):
        node_out[c : c + 1, :] = (moved[c] - found[3 + c : 4 + c]) * SCALE


SCALAR = pl.BlockSpec(memory_space=pltpu.SMEM)


def node_rates(counts, amounts, gathered, points, slot, node_place):
    return pl.pallas_call(
        node_kernel,
        out_shape=jax.ShapeDtypeStruct((3, 1024), F32),
        in_specs=[SCALAR, SCALAR, WHOLE, WHOLE, WHOLE, WHOLE],
        out_specs=WHOLE,
        scratch_shapes=[
            pltpu.VMEM((NW, 48, PB), BF),
            pltpu.VMEM((NW, 32, PB), BF),
            pltpu.VMEM((33 * TILE, 32), F32),
        ],
        compiler_params=pltpu.CompilerParams(vmem_limit_bytes=40 << 20),
        cost_estimate=pl.CostEstimate(flops=1 << 33, bytes_accessed=2 << 20, transcendentals=3 << 20),
    )(counts, amounts, gathered, points, slot, node_place)


def pair_kernel(counts, gathered, velocity_out, stretch_out, total):
    wake = lax.axis_index("wake")
    grid = lax.axis_index("grid")
    own = gathered[wake // 2, lax.rem(wake, 2), :, pl.ds(pl.multiple_of(grid * 256, 256), 256)]
    place = [own[c : c + 1] - 0.5 for c in range(3)]
    spin = [own[3 + c : 4 + c] for c in range(3)]
    weight = (
        place[0] * place[0] + place[1] * place[1] + place[2] * place[2] + 0.5 * own[6:7] * own[6:7]
    )
    rows = lax.broadcasted_iota(jnp.int32, (256, 256), 0)
    lanes = lax.broadcasted_iota(jnp.int32, (256, 256), 1)
    identity = jnp.where(rows == lanes, 1.0, 0.0).astype(BF)
    targets = dot_nt(identity, target_rows(place, weight, True)).astype(BF)
    total[...] = jnp.zeros_like(total)

    def count_items(turn, amount):
        return amount + pl.cdiv(counts[lax.rem(wake + turn + NW - 4, NW)], CHUNK)

    items = lax.fori_loop(0, NW // 2, count_items, 0)

    def run(step, carry):
        turn, chunk = carry
        gain = None
        for _ in range(PAIRED):
            block = lax.rem(wake + jnp.minimum(turn, NW // 2 - 1) + NW - 4, NW)
            start = pl.multiple_of(chunk * CHUNK, CHUNK)
            distance, moment, source, half = build_source(counts, gathered, block, start, CHUNK)
            moment = jnp.where(turn < NW // 2, moment, 0.0)
            parts = [split_three(moment)]
            for factor in (source[0], source[1], source[2], half):
                parts.append(split_three(moment * factor))
            columns = [parts[k][level] for level in range(3) for k in range(5)]
            columns = jnp.concatenate(columns + [jnp.zeros_like(moment)], axis=0).astype(BF)
            for cut in range(0, CHUNK, 256):
                squared = jnp.dot(targets, distance[:, cut : cut + 256], preferred_element_type=F32)
                root = lax.rsqrt(squared)
                second = root * root
                fifth = second * second * root
                high = fifth.astype(BF)
                low = (fifth - high.astype(F32)).astype(BF)
                added = dot_nt(jnp.concatenate([high, low], axis=0), columns[:, cut : cut + 256])
                gain = added if gain is None else gain + added
            end = chunk + 1 >= pl.cdiv(counts[block], CHUNK)
            turn = jnp.where(end, turn + 1, turn)
            chunk = jnp.where(end, 0, chunk + 1)
        total[...] += gain
        return turn, chunk

    lax.fori_loop(0, pl.cdiv(items, PAIRED), run, (0, 0))

    sums = jnp.transpose(total[0:256, :] + total[256:512, :])
    sums = sums[0:40] + sums[40:80] + sums[80:120]
    plain = [sums[k : k + 1] for k in range(6)]
    turned = [[sums[8 + 8 * c + k : 9 + 8 * c + k] for k in range(6)] for c in range(3)]
    heavy = [sums[32 + k : 33 + k] for k in range(6)]
    mixed = [
        weight * plain[k]
        + heavy[k]
        - 2.0 * (place[0] * turned[0][k] + place[1] * turned[1][k] + place[2] * turned[2][k])
        for k in range(6)
    ]
    live = grid * 256 + lax.broadcasted_iota(jnp.int32, (1, 256), 1) < counts[wake]
    factor = jnp.where(live, SCALE, 0.0)
    swept = cross_rows(place, mixed[0:3])
    bent_own = cross_rows(place, plain[0:3])
    along = spin[0] * place[0] + spin[1] * place[1] + spin[2] * place[2]
    pulled = [spin[0] * turned[0][k] + spin[1] * turned[1][k] + spin[2] * turned[2][k] for k in range(6)]
    bent_far = cross_rows(place, pulled[0:3])
    lifted = cross_rows(spin, mixed[0:3])
    for c in range(3):
        velocity_out[c : c + 1, :] = (swept[c] - mixed[3 + c]) * factor
        bent = along * (bent_own[c] - plain[3 + c]) - (bent_far[c] - pulled[3 + c])
        stretch_out[c : c + 1, :] = (lifted[c] - 3.0 * bent) * factor


def pair_rates(counts, gathered):
    return pl.pallas_call(
        pair_kernel,
        out_shape=[jax.ShapeDtypeStruct((3, 256), F32)] * 2,
        in_specs=[SCALAR, WHOLE],
        out_specs=[WHOLE] * 2,
        scratch_shapes=[pltpu.VMEM((512, 128), F32)],
        compiler_params=pltpu.CompilerParams(vmem_limit_bytes=32 << 20),
        cost_estimate=pl.CostEstimate(flops=1 << 34, bytes_accessed=2 << 20, transcendentals=3 << 20),
    )(counts, gathered)


SPAN = 1280
WIDE = 16640
BUFFER = WIDE + 256


def sweep_kernel(
    flow, sections, viscosity, below, above, left, right, nodes, out,
    rows_in, kind, first, second, rates, rows_out, sem_in, sem_out,
):
    fields = 5
    incoming = [
        pltpu.make_async_copy(flow.at[f], rows_in.at[f, pl.ds(0, 16), pl.ds(256, 16384)], sem_in.at[f])
        for f in range(fields)
    ]
    for copy in incoming:
        copy.start()
    kind[0:16, 256:16640] = sections[...].astype(F32) + 1.0
    kind[16:19, 256:16640] = below[5]
    kind[19:21, 256:16640] = jnp.zeros((2, 16384), F32)
    kind[21:24, 256:16640] = above[5]
    kind[:, 128:256] = left[5]
    kind[:, 16640:16768] = right[5]
    steps = WIDE // SPAN
    lane = lax.broadcasted_iota(jnp.int32, (8, 128), 1)

    def neighbours(wide):
        across = (pltpu.roll(wide, 1, 1) + pltpu.roll(wide, SPAN + 255, 1))[:, 128 : SPAN + 128]
        mid = wide[:, 128 : SPAN + 128]
        return mid, across + (pltpu.roll(mid, 1, 0) + pltpu.roll(mid, 23, 0))

    outgoing = []
    for f in (0, 4, 1, 2, 3):
        incoming[f].wait()
        rows_in[f, 16:19, 256:16640] = below[f]
        rows_in[f, 19:21, 256:16640] = jnp.zeros((2, 16384), F32)
        rows_in[f, 21:24, 256:16640] = above[f]
        rows_in[f, :, 128:256] = left[f]
        rows_in[f, :, 16640:16768] = right[f]

        if f in (1, 2, 3):
            for k in range(65):
                start = 256 + 256 * k
                for tile in range(3):
                    where = (f, pl.ds(8 * tile, 8), pl.ds(start, 128))
                    column = jnp.broadcast_to(nodes[f - 1, 8 * tile : 8 * tile + 8, k : k + 1], (8, 128))
                    rows_in[where] = jnp.where(lane == 0, column, rows_in[where])

        def sweep_first(step, carry):
            start = pl.multiple_of(step * SPAN, 128)
            inner = pl.ds(pl.multiple_of(start + 128, 128), SPAN)
            mid, beside = neighbours(rows_in[f, :, pl.ds(start, SPAN + 256)])
            name = kind[:, inner]
            rate = jnp.where(
                name == 1.0,
                viscosity[0, f],
                jnp.where(name == 2.0, viscosity[1, f], jnp.where(name == 3.0, viscosity[2, f], 0.0)),
            )
            rates[:, inner] = rate
            first[:, inner] = mid + rate * (beside - 4.0 * mid)
            return carry

        def sweep_second(step, carry):
            start = pl.multiple_of(step * SPAN, 128)
            inner = pl.ds(pl.multiple_of(start + 128, 128), SPAN)
            mid, beside = neighbours(first[:, pl.ds(start, SPAN + 256)])
            second[:, inner] = mid + rates[:, inner] * (beside - 4.0 * mid)
            return carry

        def sweep_third(step, carry):
            start = pl.multiple_of(step * SPAN, 128)
            inner = pl.ds(pl.multiple_of(start + 128, 128), SPAN)
            mid, beside = neighbours(second[:, pl.ds(start, SPAN + 256)])
            rows_out[f, :, inner] = (mid + rates[:, inner] * (beside - 4.0 * mid))[0:16]
            return carry

        lax.fori_loop(0, steps, sweep_first, 0)
        lax.fori_loop(0, steps, sweep_second, 0)
        lax.fori_loop(0, steps, sweep_third, 0)
        copy = pltpu.make_async_copy(
            rows_out.at[f, :, pl.ds(256, 16384)], out.at[f], sem_out.at[f]
        )
        copy.start()
        outgoing.append(copy)
    for copy in outgoing:
        copy.wait()


def sweep_fields(flow, sections, viscosity, below, above, left, right, nodes):
    return pl.pallas_call(
        sweep_kernel,
        out_shape=jax.ShapeDtypeStruct((5, 16, 16384), F32),
        in_specs=[pl.BlockSpec(memory_space=pl.ANY), WHOLE, SCALAR] + [WHOLE] * 5,
        out_specs=pl.BlockSpec(memory_space=pl.ANY),
        scratch_shapes=[
            pltpu.VMEM((5, 24, BUFFER), F32),
            pltpu.VMEM((24, BUFFER), F32),
            pltpu.VMEM((24, BUFFER), F32),
            pltpu.VMEM((24, BUFFER), F32),
            pltpu.VMEM((24, BUFFER), F32),
            pltpu.VMEM((5, 16, BUFFER), F32),
            pltpu.SemaphoreType.DMA((5,)),
            pltpu.SemaphoreType.DMA((5,)),
        ],
        compiler_params=pltpu.CompilerParams(vmem_limit_bytes=56 << 20),
        cost_estimate=pl.CostEstimate(flops=1 << 25, bytes_accessed=14 << 20, transcendentals=0),
    )(flow, sections, viscosity, below, above, left, right, nodes)


def shift(value, wake_by, grid_by):
    pairs = []
    for wake in range(NW):
        for grid in range(NG):
            to_wake, to_grid = wake + wake_by, grid + grid_by
            if 0 <= to_wake < NW and 0 <= to_grid < NG:
                pairs.append((wake * NG + grid, to_wake * NG + to_grid))
    return lax.ppermute(value, ("wake", "grid"), pairs)


def on_device(
    flow,
    section_map,
    viscosity,
    particle_position,
    particle_strength,
    particle_core,
    shed_counts,
    node_position,
    node_block,
):
    named = section_map.astype(F32)[None] + 1.0
    below = shift(jnp.concatenate([flow[:, 0:3], named[:, 0:3]], axis=0), -1, 0)
    above = shift(jnp.concatenate([flow[:, 13:16], named[:, 13:16]], axis=0), 1, 0)

    def side(lanes):
        own = jnp.concatenate([flow[:, :, lanes], named[:, :, lanes]], axis=0)
        gap = jnp.zeros((6, 2, 128), F32)
        return jnp.concatenate([own, below[:, :, lanes], gap, above[:, :, lanes]], axis=1)

    right = shift(side(slice(0, 128)), 0, -1)
    left = shift(side(slice(16256, 16384)), 0, 1)

    gathered, points, slot, amounts = gather_particles(
        particle_position, particle_strength, particle_core[None], node_position, node_block.reshape(1, 1024)
    )
    moved = node_rates(shed_counts, amounts[:, 0:1], gathered, points, slot, node_position)
    own = moved.reshape(3, 16, 64)
    corner = own[:, :, 0]
    lower = shift(own[:, 0:3], -1, 0)
    upper = shift(own[:, 13:16], 1, 0)
    beside = shift(corner, 0, -1)
    beside_lower = shift(corner[:, 0:3], -1, -1)
    beside_upper = shift(corner[:, 13:16], 1, -1)
    gap = jnp.zeros((3, 2, 65), F32)

    def joined(rows, column):
        return jnp.concatenate([rows, column[:, :, None]], axis=2)

    nodes = jnp.concatenate(
        [joined(own, beside), joined(lower, beside_lower), gap, joined(upper, beside_upper)], axis=1
    )
    nodes = jnp.pad(nodes, ((0, 0), (0, 0), (0, 63)))
    velocity, stretch = pair_rates(shed_counts, gathered)
    field = sweep_fields(flow, section_map, viscosity, below, above, left, right, nodes)
    return (field, velocity, stretch)


def solution(mesh):
    return jax.shard_map(
        on_device,
        mesh=mesh,
        in_specs=(
            P(None, "wake", "grid"),
            P("wake", "grid"),
            P(),
            P(None, ("wake", "grid")),
            P(None, ("wake", "grid")),
            P(("wake", "grid")),
            P(),
            P(None, ("wake", "grid")),
            P(("wake", "grid"), None),
        ),
        out_specs=(P(None, "wake", "grid"), P(None, ("wake", "grid")), P(None, ("wake", "grid"))),
        check_vma=False,
    )
```

time: 872 us -> 143 us (0.16); the launches traced: 857 us -> 141 us
  other arithmetic: 422 us -> 3.24 us
  local copies, waits for them, and re-layouts: 277 us -> 11.5 us
  Pallas kernels: 0 us -> 89 us
  starting transfers between devices: 105 us -> 34.3 us
  waiting for transfers between devices: 27.4 us -> 1.91 us
  blocking collectives: 22.6 us -> 0 us
    scatter x128 -> x0, other arithmetic: 291 us -> none
    scatter x194 -> x0, local copies, waits for them, and re-layouts: 229 us -> none
    pallas_call x0 -> x4, Pallas kernels: none -> 89 us  [the longest x1 32.9 us: sweep_fields(): pl.pallas_call(sweep_kernel, out_shape=jax.ShapeDtypeStruct((5, 16, 16384...]
    reduce_sum x17 -> x0, other arithmetic: 63.4 us -> none  [the longest x8 39.1 us: particle_rates(): jnp.sum(steep * along * curl[component], axis=1)]
    ppermute x20 -> x9, starting transfers between devices: 90.8 us -> 34.3 us  [shift(): return lax.ppermute(value, ('wake', 'grid'), pairs)]
    add x10 -> x1, other arithmetic: 39.6 us -> 0.07 us  [on_device(): named = section_map.astype(F32)[None] + 1.0]
    ppermute x20 -> x9, waiting for transfers between devices: 27.4 us -> 1.91 us  [shift(): return lax.ppermute(value, ('wake', 'grid'), pairs)]
    all_gather x1 -> x0, blocking collectives: 22.6 us -> none  [on_device(): block = lax.all_gather(share, 'grid', axis=1, tiled=True)]
  transfers between devices with their start and end apart: 22 -> 9, of which waited for: 8 -> 1; matrix products, arithmetic and copies ran while one was open for 73% -> 6% of each run, Pallas kernels for 0% -> 8%
where the time goes in v1:
time: 143 us; the launch traced here: 141 us
  Pallas kernels  89 us (62%)
  starting transfers between devices  34.3 us (24%)
  local copies, waits for them, and re-layouts  11.5 us (8%)
  other arithmetic  3.24 us (2%)
  waiting for transfers between devices  1.91 us (1%)
    ppermute x9, starting transfers between devices, shift(): return lax.ppermute(value, ('wake', 'grid'), pairs)  34.3 us
    pallas_call x1, Pallas kernels, sweep_fields(): pl.pallas_call(sweep_kernel, out_shape=jax.ShapeDtypeStruct((5, 16, 16384...  32.9 us
    pallas_call x1, Pallas kernels, node_rates(): pl.pallas_call(node_kernel, out_shape=jax.ShapeDtypeStruct((3, 1024), F32...  25.7 us
    pallas_call x1, Pallas kernels, gather_particles(): pl.pallas_call(gather_kernel, out_shape=[jax.ShapeDtypeStruct((NW // 2, 2...  19.7 us
    pallas_call x1, Pallas kernels, pair_rates(): pl.pallas_call(pair_kernel, out_shape=[jax.ShapeDtypeStruct((3, 256), F32...  10.7 us
    unnamed x24, local copies, waits for them, and re-layouts  5.46 us
    slice x1, local copies, waits for them, and re-layouts, on_device(): flow[:, 13:16]  3.03 us
  transfers between devices with their start and end apart: 9, of which 1 were waited for; matrix products, arithmetic and copies ran while one was open for 6% of the time, Pallas kernels for 8%

profile of v1, /device:TPU:39, one launch (start us, length us, event | category | flops | bytes accessed | tf_op | source)
XLA Modules:
  0.0 140.8 jit_solution(1219754520602103611)
XLA Ops:
  0.6 0.0 copy-start
  0.6 0.7 copy-done
  1.4 0.0 copy-start.2
  1.4 0.7 copy-done.2
  2.0 0.0 copy-start.3
  2.0 0.7 copy-done.3
  2.7 0.0 copy-start.4
  2.7 0.7 copy-done.4
  3.4 0.0 copy-start.5
  3.4 0.7 copy-done.5
  4.1 19.7 %shard_map.112 = (f32[8,2,8,2048]{3,2,1,0:T(8,128)S(1)}, bf16[2048,48]{1,0:T(8,128)(2,1)S(1)}, s32[1,1024]{1,0:T(1,128)S(1)}, s32[16,128]{1,0:T(8,128)S(1)}) custom-call(f32[3,256]{1,0:T(4,128)S(1)} %copy-done.2, f32[3,256]{1,0:T(4,128)S(1)} %copy-done.3, f32[1,256]{1,0:T(1,128)S(1)} %bitcast.9, f32[3,1024]{1,0:T(4,128)S(1)} %copy-done, s32[1,1024]{1,0:T(1,128)S(1)} %bitcast.8), custom_call_target="tpu_custom_call" | custom-call | flops 268435456 | bytes 4194304 | tf_op jit(solution)/shard_map/pallas_call | solution.py:173
  23.8 0.0 copy-start.1
  23.8 0.7 copy-done.1
  24.5 0.0 copy-start.6
  24.5 0.7 copy-done.6
  25.2 0.0 copy-start.8
  25.2 25.7 %shard_map.113 = f32[3,1024]{1,0:T(4,128)S(1)} custom-call(s32[16]{0:T(128)S(1)} %copy-done.6, s32[16,1]{1,0:T(8,128)S(1)} %bitcast.10, f32[8,2,8,2048]{3,2,1,0:T(8,128)S(1)} %get-tuple-element.10.gathered, bf16[2048,48]{1,0:T(8,128)(2,1)S(1)} %get-tuple-element.11.points, s32[1,1024]{1,0:T(1,128)S(1)} %get-tuple-element.12.slot, f32[3,1024]{1,0:T(4,128)S(1)} %copy-done.1), custom_call_target="tpu_custom_call" | custom-call | flops 8589934592 | bytes 2097152 | tf_op jit(solution)/shard_map/pallas_call | solution.py:295
  50.9 0.1 reshape.14
  51.0 0.1 slice_reduce_fusion
  51.1 2.5 %collective-permute-start.4 = (f32[3,16]{1,0:T(4,128)S(1)}, f32[3,16]{1,0:T(4,128)S(1)}, u32[]{:S(2)}, u32[]{:S(2)}) collective-permute-start(f32[3,16]{1,0:T(4,128)S(1)} %slice_reduce_fusion), channel_id=1, source_target_pairs={{1,0},{2,1},{3,2},{4,3},{5,4},{6,5},{7,6},{9,8},{10,9},{11,10},{12... | collective-permute-start | bytes 584 | tf_op jit(solution)/shard_map/ppermute | solution.py:512
  53.6 0.1 fusion.7
  53.7 3.6 %collective-permute-start.6 = (f32[3,3]{1,0:T(4,128)S(1)}, f32[3,3]{1,0:T(4,128)S(1)}, u32[]{:S(2)}, u32[]{:S(2)}) collective-permute-start(f32[3,3]{1,0:T(4,128)S(1)} %get-tuple-element.29), channel_id=1, source_target_pairs={{9,0},{10,1},{11,2},{12,3},{13,4},{14,5},{15,6},{17,8},{18,9},{19,... | collective-permute-start | bytes 116 | tf_op jit(solution)/shard_map/ppermute | solution.py:512
  57.3 4.6 %collective-permute-start.8 = (f32[3,3]{1,0:T(4,128)S(1)}, f32[3,3]{1,0:T(4,128)S(1)}, u32[]{:S(2)}, u32[]{:S(2)}) collective-permute-start(f32[3,3]{1,0:T(4,128)S(1)} %get-tuple-element.30), channel_id=1, source_target_pairs={{1,8},{2,9},{3,10},{4,11},{5,12},{6,13},{7,14},{9,16},{10,17},{11,... | collective-permute-start | bytes 116 | tf_op jit(solution)/shard_map/ppermute | solution.py:512
  61.9 0.0 copy-done.8
  61.9 0.1 add_bitcast_fusion
  62.0 0.1 fusion.5
  62.1 3.0 %fusion.1 = (f32[5,3,16384]{2,1,0:T(4,128)S(1)}, f32[5,3,16384]{2,1,0:T(4,128)S(1)}) fusion(f32[5,16,16384]{2,1,0:T(8,128)} %flow.1), kind=kLoop, calls=%fused_computation.8 | loop fusion | bytes 3932160 | tf_op jit(solution)/shard_map/slice | solution.py:528
  65.1 1.5 %pad_maximum_fusion = f32[6,3,16384]{2,1,0:T(4,128)} fusion(f32[1,3,16384]{2,1,0:T(4,128)S(1)} %get-tuple-element.26, f32[5,3,16384]{2,1,0:T(4,128)S(1)} %get-tuple-element.18), kind=kLoop, calls=%fused_computation | loop fusion | flops 294912 | bytes 2359296 | tf_op jit(solution)/shard_map/concatenate | solution.py:527
  66.6 1.9 %collective-permute-start = (f32[6,3,16384]{2,1,0:T(4,128)}, f32[6,3,16384]{2,1,0:T(4,128)S(1)}, u32[]{:S(2)}, u32[]{:S(2)}) collective-permute-start(f32[6,3,16384]{2,1,0:T(4,128)} %pad_maximum_fusion), channel_id=1, source_target_pairs={{8,0},{9,1},{10,2},{11,3},{12,4},{13,5},{14,6},{15,7},{16,8},{17,9... | collective-permute-start | bytes 3538952 | tf_op jit(solution)/shard_map/ppermute | solution.py:512
  68.5 0.0 copy-start.7
  68.5 1.5 %pad_maximum_fusion.1 = f32[6,3,16384]{2,1,0:T(4,128)} fusion(f32[1,3,16384]{2,1,0:T(4,128)S(1)} %get-tuple-element.25, f32[5,3,16384]{2,1,0:T(4,128)S(1)} %get-tuple-element.17), kind=kLoop, calls=%fused_computation.1 | loop fusion | flops 294912 | bytes 2359296 | tf_op jit(solution)/shard_map/concatenate | solution.py:528
  70.1 7.2 %collective-permute-start.1 = (f32[6,3,16384]{2,1,0:T(4,128)}, f32[6,3,16384]{2,1,0:T(4,128)}, u32[]{:S(2)}, u32[]{:S(2)}) collective-permute-start(f32[6,3,16384]{2,1,0:T(4,128)} %pad_maximum_fusion.1), channel_id=1, source_target_pairs={{0,8},{1,9},{2,10},{3,11},{4,12},{5,13},{6,14},{7,15},{8,16},{9,17... | collective-permute-start | bytes 3538952 | tf_op jit(solution)/shard_map/ppermute | solution.py:512
  77.3 0.8 fusion
  78.1 0.1 pad.20.clone
  78.2 0.0 copy-done.7
  78.2 10.7 %shard_map.115 = (f32[3,256]{1,0:T(4,128)}, f32[3,256]{1,0:T(4,128)}) custom-call(s32[16]{0:T(128)S(1)} %copy-done.7, f32[8,2,8,2048]{3,2,1,0:T(8,128)S(1)} %get-tuple-element.10.gathered), custom_call_target="tpu_custom_call" | custom-call | flops 17179869184 | bytes 2097152 | tf_op jit(solution)/shard_map/pallas_call | solution.py:386
  88.9 0.0 collective-permute-done.6
  88.9 1.9 %collective-permute-start.5 = (f32[3,3,64]{2,1,0:T(4,128)S(1)}, f32[3,3,64]{2,1,0:T(4,128)S(1)}, u32[]{:S(2)}, u32[]{:S(2)}) collective-permute-start(f32[3,3,64]{2,1,0:T(4,128)S(1)} %get-tuple-element.27), channel_id=1, source_target_pairs={{8,0},{9,1},{10,2},{11,3},{12,4},{13,5},{14,6},{15,7},{16,8},{17,9... | collective-permute-start | bytes 6920 | tf_op jit(solution)/shard_map/ppermute | solution.py:512
  90.8 0.1 copy.16
  90.9 0.0 collective-permute-done.8
  90.9 7.2 %collective-permute-start.7 = (f32[3,3,64]{2,1,0:T(4,128)S(1)}, f32[3,3,64]{2,1,0:T(4,128)S(1)}, u32[]{:S(2)}, u32[]{:S(2)}) collective-permute-start(f32[3,3,64]{2,1,0:T(4,128)S(1)} %get-tuple-element.28), channel_id=1, source_target_pairs={{0,8},{1,9},{2,10},{3,11},{4,12},{5,13},{6,14},{7,15},{8,16},{9,17... | collective-permute-start | bytes 6920 | tf_op jit(solution)/shard_map/ppermute | solution.py:512
  98.2 0.1 copy.17
  98.3 0.0 collective-permute-done.4
  98.3 0.1 copy.15
  98.4 0.0 collective-permute-done.below
  98.4 0.0 copy-start.9
  98.4 0.0 collective-permute-done.1.above
  98.4 0.8 fusion.3
  99.3 0.1 pad_maximum_fusion.3
  99.3 1.9 %collective-permute-start.3 = (f32[6,24,128]{2,1,0:T(8,128)S(1)}, f32[6,24,128]{2,1,0:T(8,128)S(1)}, u32[]{:S(2)}, u32[]{:S(2)}) collective-permute-start(f32[6,24,128]{2,1,0:T(8,128)S(1)} %get-tuple-element.31), channel_id=1, source_target_pairs={{1,0},{2,1},{3,2},{4,3},{5,4},{6,5},{7,6},{9,8},{10,9},{11,10},{12... | collective-permute-start | bytes 221192 | tf_op jit(solution)/shard_map/ppermute | solution.py:512
  101.3 3.4 %collective-permute-start.2 = (f32[6,24,128]{2,1,0:T(8,128)S(1)}, f32[6,24,128]{2,1,0:T(8,128)S(1)}, u32[]{:S(2)}, u32[]{:S(2)}) collective-permute-start(f32[6,24,128]{2,1,0:T(8,128)S(1)} %get-tuple-element.32), channel_id=1, source_target_pairs={{0,1},{1,2},{2,3},{3,4},{4,5},{5,6},{6,7},{8,9},{9,10},{10,11},{11... | collective-permute-start | bytes 221192 | tf_op jit(solution)/shard_map/ppermute | solution.py:512
  104.6 0.0 collective-permute-done.5
  104.6 0.0 collective-permute-done.7
  104.7 0.1 maximum_maximum_fusion
  104.7 0.6 pad.4.nodes
  105.4 0.0 collective-permute-done.3.right
  105.4 0.0 copy-start.10
  105.4 1.9 %collective-permute-done.2.left = f32[6,24,128]{2,1,0:T(8,128)S(1)} collective-permute-done((f32[6,24,128]{2,1,0:T(8,128)S(1)}, f32[6,24,128]{2,1,0:T(8,128)S(1)}, u32[]{:S(2)}, u32[]{:S(2)}) %collective-permute-start.2) | collective-permute-done | bytes 73760 | tf_op jit(solution)/shard_map/ppermute | solution.py:512
  107.3 0.0 copy-done.9
  107.3 0.0 copy-done.10
  107.3 0.0 copy-start.11
  107.3 0.6 copy-done.11
  107.9 32.9 %shard_map.114 = f32[5,16,16384]{2,1,0:T(8,128)} custom-call(f32[5,16,16384]{2,1,0:T(8,128)} %flow.1, s32[16,16384]{1,0:T(8,128)} %sections.1, f32[3,5]{1,0:T(4,128)} %viscosity.1, f32[6,3,16384]{2,1,0:T(4,128)} %copy-done.9, f32[6,3,16384]{2,1,0:T(4,128)} %collective-permute-done.1.above, f32[6,24,128]{2,1,0:T(8,128)} %copy-done.11, ...), custom_call_target="tpu_custom_call" | custom-call | flops 33554432 | bytes 14680064 | tf_op jit(solution)/shard_map/pallas_call | solution.py:485
  (4 shorter events, 0.0 us)
Async XLA Ops:
  0.6 0.7 copy-start
  1.4 0.7 copy-start.2
  2.0 0.7 copy-start.3
  2.7 0.7 copy-start.4
  3.4 0.7 copy-start.5
  23.8 0.7 copy-start.1
  24.5 0.7 copy-start.6
  25.2 36.7 %copy-start.8 = (s32[16,16384]{1,0:T(8,128)S(1)}, s32[16,16384]{1,0:T(8,128)}, u32[]{:S(2)}) copy-start(s32[16,16384]{1,0:T(8,128)} %sections.1) | copy-start | bytes 3145732
  51.1 47.2 %collective-permute-start.4 = (f32[3,16]{1,0:T(4,128)S(1)}, f32[3,16]{1,0:T(4,128)S(1)}, u32[]{:S(2)}, u32[]{:S(2)}) collective-permute-start(f32[3,16]{1,0:T(4,128)S(1)} %slice_reduce_fusion), channel_id=1, source_target_pairs={{1,0},{2,1},{3,2},{4,3},{5,4},{6,5},{7,6},{9,8},{10,9},{11,10},{12... | collective-permute-start | bytes 584 | tf_op jit(solution)/shard_map/ppermute | solution.py:512
  53.7 35.2 %collective-permute-start.6 = (f32[3,3]{1,0:T(4,128)S(1)}, f32[3,3]{1,0:T(4,128)S(1)}, u32[]{:S(2)}, u32[]{:S(2)}) collective-permute-start(f32[3,3]{1,0:T(4,128)S(1)} %get-tuple-element.29), channel_id=1, source_target_pairs={{9,0},{10,1},{11,2},{12,3},{13,4},{14,5},{15,6},{17,8},{18,9},{19,... | collective-permute-start | bytes 116 | tf_op jit(solution)/shard_map/ppermute | solution.py:512
  57.3 33.6 %collective-permute-start.8 = (f32[3,3]{1,0:T(4,128)S(1)}, f32[3,3]{1,0:T(4,128)S(1)}, u32[]{:S(2)}, u32[]{:S(2)}) collective-permute-start(f32[3,3]{1,0:T(4,128)S(1)} %get-tuple-element.30), channel_id=1, source_target_pairs={{1,8},{2,9},{3,10},{4,11},{5,12},{6,13},{7,14},{9,16},{10,17},{11,... | collective-permute-start | bytes 116 | tf_op jit(solution)/shard_map/ppermute | solution.py:512
  66.6 31.8 %collective-permute-start = (f32[6,3,16384]{2,1,0:T(4,128)}, f32[6,3,16384]{2,1,0:T(4,128)S(1)}, u32[]{:S(2)}, u32[]{:S(2)}) collective-permute-start(f32[6,3,16384]{2,1,0:T(4,128)} %pad_maximum_fusion), channel_id=1, source_target_pairs={{8,0},{9,1},{10,2},{11,3},{12,4},{13,5},{14,6},{15,7},{16,8},{17,9... | collective-permute-start | bytes 3538952 | tf_op jit(solution)/shard_map/ppermute | solution.py:512
  68.5 9.7 %copy-start.7 = (s32[16]{0:T(128)S(1)}, s32[16]{0:T(128)}, u32[]{:S(2)}) copy-start(s32[16]{0:T(128)} %counts.3) | copy-start | bytes 196
  70.1 28.4 %collective-permute-start.1 = (f32[6,3,16384]{2,1,0:T(4,128)}, f32[6,3,16384]{2,1,0:T(4,128)}, u32[]{:S(2)}, u32[]{:S(2)}) collective-permute-start(f32[6,3,16384]{2,1,0:T(4,128)} %pad_maximum_fusion.1), channel_id=1, source_target_pairs={{0,8},{1,9},{2,10},{3,11},{4,12},{5,13},{6,14},{7,15},{8,16},{9,17... | collective-permute-start | bytes 3538952 | tf_op jit(solution)/shard_map/ppermute | solution.py:512
  88.9 15.7 %collective-permute-start.5 = (f32[3,3,64]{2,1,0:T(4,128)S(1)}, f32[3,3,64]{2,1,0:T(4,128)S(1)}, u32[]{:S(2)}, u32[]{:S(2)}) collective-permute-start(f32[3,3,64]{2,1,0:T(4,128)S(1)} %get-tuple-element.27), channel_id=1, source_target_pairs={{8,0},{9,1},{10,2},{11,3},{12,4},{13,5},{14,6},{15,7},{16,8},{17,9... | collective-permute-start | bytes 6920 | tf_op jit(solution)/shard_map/ppermute | solution.py:512
  90.9 13.7 %collective-permute-start.7 = (f32[3,3,64]{2,1,0:T(4,128)S(1)}, f32[3,3,64]{2,1,0:T(4,128)S(1)}, u32[]{:S(2)}, u32[]{:S(2)}) collective-permute-start(f32[3,3,64]{2,1,0:T(4,128)S(1)} %get-tuple-element.28), channel_id=1, source_target_pairs={{0,8},{1,9},{2,10},{3,11},{4,12},{5,13},{6,14},{7,15},{8,16},{9,17... | collective-permute-start | bytes 6920 | tf_op jit(solution)/shard_map/ppermute | solution.py:512
  98.4 8.9 %copy-start.9 = (f32[6,3,16384]{2,1,0:T(4,128)}, f32[6,3,16384]{2,1,0:T(4,128)S(1)}, u32[]{:S(2)}) copy-start(f32[6,3,16384]{2,1,0:T(4,128)S(1)} %collective-permute-done.below) | copy-start | bytes 3538948
  99.3 6.0 %collective-permute-start.3 = (f32[6,24,128]{2,1,0:T(8,128)S(1)}, f32[6,24,128]{2,1,0:T(8,128)S(1)}, u32[]{:S(2)}, u32[]{:S(2)}) collective-permute-start(f32[6,24,128]{2,1,0:T(8,128)S(1)} %get-tuple-element.31), channel_id=1, source_target_pairs={{1,0},{2,1},{3,2},{4,3},{5,4},{6,5},{7,6},{9,8},{10,9},{11,10},{12... | collective-permute-start | bytes 221192 | tf_op jit(solution)/shard_map/ppermute | solution.py:512
  101.3 6.0 %collective-permute-start.2 = (f32[6,24,128]{2,1,0:T(8,128)S(1)}, f32[6,24,128]{2,1,0:T(8,128)S(1)}, u32[]{:S(2)}, u32[]{:S(2)}) collective-permute-start(f32[6,24,128]{2,1,0:T(8,128)S(1)} %get-tuple-element.32), channel_id=1, source_target_pairs={{0,1},{1,2},{2,3},{3,4},{4,5},{5,6},{6,7},{8,9},{9,10},{10,11},{11... | collective-permute-start | bytes 221192 | tf_op jit(solution)/shard_map/ppermute | solution.py:512
  105.4 1.9 %copy-start.10 = (f32[6,24,128]{2,1,0:T(8,128)}, f32[6,24,128]{2,1,0:T(8,128)S(1)}, u32[]{:S(2)}) copy-start(f32[6,24,128]{2,1,0:T(8,128)S(1)} %collective-permute-done.3.right) | copy-start | bytes 221188
  107.3 0.6 copy-start.11

commit v2 on v0

v2 whole, which is shorter than its diff:
```python
import math

import jax
import jax.numpy as jnp
from jax import lax
from jax.experimental import pallas as pl
from jax.experimental.pallas import tpu as pltpu
from jax.sharding import PartitionSpec as P

PB = 2048
NW = 16
NG = 8
CHUNK = 512
BF = jnp.bfloat16
F32 = jnp.float32
MESH = pl.DeviceIdType.MESH
SCALE = -1.0 / (4.0 * math.pi)
WHOLE = pl.BlockSpec(memory_space=pltpu.VMEM)


def split_three(value):
    high = value.astype(BF).astype(F32)
    rest = value - high
    middle = rest.astype(BF).astype(F32)
    return high, middle, rest - middle


def dot_nt(first, second):
    return lax.dot_general(first, second, (((1,), (1,)), ((), ())), preferred_element_type=F32)


def cross_rows(first, second):
    return [
        first[1] * second[2] - first[2] * second[1],
        first[2] * second[0] - first[0] * second[2],
        first[0] * second[1] - first[1] * second[0],
    ]


def target_rows(place, weight, halved):
    ones = jnp.ones_like(weight)
    none = jnp.zeros_like(weight)
    parts = split_three(jnp.concatenate([-2.0 * row for row in place] + [none, none, weight, none, none], axis=0))
    unit = jnp.concatenate([none] * 3 + [none if halved else ones, ones if halved else none] + [none] * 3, axis=0)
    high, middle, low = parts
    return jnp.concatenate([high + unit, middle, low, high + unit, middle, high + unit], axis=0).astype(BF)


def source_rows(rows, live):
    place = rows[0:3]
    square = place[0] * place[0] + place[1] * place[1] + place[2] * place[2]
    core = rows[6] * rows[6]
    half = square + 0.5 * core
    ones = jnp.ones_like(square)
    none = jnp.zeros_like(square)
    high, middle, low = split_three(
        jnp.concatenate(list(place) + [square + core, half, ones, none, none], axis=0)
    )
    distance = jnp.concatenate([high, high, high, middle, middle, low], axis=0).astype(BF)
    spin = [jnp.where(live, rows[3 + c], 0.0) for c in range(3)]
    moment = jnp.concatenate(spin + cross_rows(place, spin) + [none, none], axis=0)
    return distance, moment, half


def source_columns(moment, factors):
    parts = [split_three(moment)] + [split_three(moment * factor) for factor in factors]
    columns = [part[level] for level in range(3) for part in parts]
    return columns


def centred(rows):
    return [rows[c : c + 1] - 0.5 for c in range(3)]


def square_sum(place):
    return place[0] * place[0] + place[1] * place[1] + place[2] * place[2]


def gather_kernel(
    counts, place_in, spin_in, core_in, node_place_in, node_block_in, flow, sections,
    velocity_out, stretch_out, own_nodes, far_nodes, rows_halo, left_halo, right_halo,
    kind_rows, kind_left, kind_right,
    gathered, share, node_place, node_block, points, targets_ref, total, node_total, answers,
    sem_in, send_one, recv_one, send_two, recv_two, send_three, recv_three,
    send_halo, recv_halo, send_node, recv_node,
):
    wake = lax.axis_index("wake")
    grid = lax.axis_index("grid")
    side = lax.rem(wake, 2)
    pair = wake // 2
    lanes = pl.ds(pl.multiple_of(grid * 256, 256), 256)
    mine = gathered.at[pair, side, :, lanes]

    def device(wake_by, grid_by):
        return {"wake": lax.rem(wake + wake_by + NW, NW), "grid": lax.rem(grid + grid_by + NG, NG)}

    loads = [
        pltpu.make_async_copy(source, target, sem_in.at[k])
        for k, (source, target) in enumerate(
            [
                (place_in, share.at[0]),
                (spin_in, share.at[1]),
                (core_in, share.at[2, pl.ds(0, 1)]),
                (node_place_in, node_place),
                (node_block_in, node_block),
            ]
        )
    ]
    for load in loads:
        load.start()

    peers = [(0, turn) for turn in range(1, NG)] + [(2 * turn, 0) for turn in range(1, NG)]
    peers += [(1, 0), (-1, 0), (1, 1), (1, -1), (-1, 1), (-1, -1)]
    barrier = pltpu.get_barrier_semaphore()
    for peer in peers:
        pl.semaphore_signal(barrier, inc=1, device_id=device(*peer), device_id_type=MESH)
    for load in loads:
        load.wait()
    mine[...] = jnp.concatenate(
        [share[0], share[1], share[2, 0:1], jnp.zeros((1, 256), F32)], axis=0
    )
    pl.semaphore_wait(barrier, len(peers))

    def send(source, target, sends, recvs, slot, peer):
        copy = pltpu.make_async_remote_copy(
            src_ref=source,
            dst_ref=target,
            send_sem=sends.at[slot],
            recv_sem=recvs.at[slot],
            device_id=device(*peer),
            device_id_type=MESH,
        )
        copy.start()
        return copy

    first = [send(mine, mine, send_one, recv_one, turn - 1, (0, turn)) for turn in range(1, NG)]

    names = node_block[...]
    spots = centred(node_place)
    rows = target_rows(spots, square_sum(spots), False)
    members = jnp.where(lax.broadcasted_iota(jnp.int32, (NW, 1024), 0) == names, 1.0, 0.0)
    triangle = jnp.where(
        lax.broadcasted_iota(jnp.int32, (128, 128), 0) <= lax.broadcasted_iota(jnp.int32, (128, 128), 1),
        1.0,
        0.0,
    ).astype(BF)
    pieces = jnp.concatenate([members[:, 128 * k : 128 * (k + 1)] for k in range(8)], axis=0)
    running = jnp.dot(pieces.astype(BF), triangle, preferred_element_type=F32)
    before = jnp.zeros((NW, 1), F32)
    ranks = []
    for k in range(8):
        part = running[NW * k : NW * (k + 1)]
        ranks.append(part + before)
        before = before + part[:, 127:128]
    rank = jnp.sum(members * jnp.concatenate(ranks, axis=1), axis=0, keepdims=True) - 1.0
    slot = names * 128 + rank.astype(jnp.int32)

    own = mine[...]
    place = centred(own)
    weight = square_sum(place) + 0.5 * own[6:7] * own[6:7]
    identity = jnp.where(
        lax.broadcasted_iota(jnp.int32, (256, 256), 0) == lax.broadcasted_iota(jnp.int32, (256, 256), 1),
        1.0,
        0.0,
    ).astype(BF)
    targets_ref[...] = dot_nt(identity, target_rows(place, weight, True)).astype(BF)
    total[...] = jnp.zeros_like(total)

    for copy in first:
        copy.wait_recv()
    block_here = gathered.at[pair, side]
    second = [
        send(block_here, block_here, send_two, recv_two, turn - 1, (2 * turn, 0)) for turn in range(1, NG)
    ]

    top, bottom = pl.ds(0, 3), pl.ds(13, 3)
    low_rows, high_rows = pl.ds(0, 3), pl.ds(5, 3)
    begin, finish = pl.ds(0, 128), pl.ds(16256, 128)
    middle, before_lanes, after_lanes = pl.ds(256, 16384), pl.ds(128, 128), pl.ds(16640, 128)
    everything, every = pl.ds(0, 16384), pl.ds(0, 16)
    plan = [
        ((-1, 0), top, everything, 0, low_rows, middle),
        ((1, 0), bottom, everything, 0, high_rows, middle),
        ((0, -1), every, begin, 2, every, begin),
        ((0, 1), every, finish, 1, every, begin),
        ((-1, -1), top, begin, 0, low_rows, after_lanes),
        ((-1, 1), top, finish, 0, low_rows, before_lanes),
        ((1, -1), bottom, begin, 0, high_rows, after_lanes),
        ((1, 1), bottom, finish, 0, high_rows, before_lanes),
    ]
    halos = []
    for k, (peer, from_rows, from_lanes, which, to_rows, to_lanes) in enumerate(plan):
        target = (rows_halo, left_halo, right_halo)[which]
        halos.append(
            send(
                flow.at[:, from_rows, from_lanes], target.at[:, to_rows, to_lanes],
                send_halo, recv_halo, 2 * k, peer,
            )
        )
        target = (kind_rows, kind_left, kind_right)[which]
        halos.append(
            send(
                sections.at[from_rows, from_lanes], target.at[to_rows, to_lanes],
                send_halo, recv_halo, 2 * k + 1, peer,
            )
        )

    def place_nodes(part, carry):
        start = pl.multiple_of(part * 256, 256)
        chosen = jnp.where(
            lax.broadcasted_iota(jnp.int32, (256, 1024), 0) + part * 256 == slot, 1.0, 0.0
        ).astype(BF)
        points[pl.ds(start, 256), :] = dot_nt(chosen, rows).astype(BF)
        return carry

    lax.fori_loop(0, 8, place_nodes, 0)

    def load_source(block, start):
        tile = gathered[block // 2, lax.rem(block, 2), :, pl.ds(start, CHUNK)]
        live = start + lax.broadcasted_iota(jnp.int32, (1, CHUNK), 1) < counts[block]
        source = centred(tile) + [tile[c : c + 1] for c in range(3, 7)]
        distance, moment, half = source_rows(source, live)
        return distance, moment, source[0:3] + [half]

    def node_slots(block):
        return pl.ds(pl.multiple_of(block * 128, 128), 128)

    def split_two(value):
        high = value.astype(BF)
        return high, (value - high.astype(F32)).astype(BF)

    def near(offset):
        block = lax.rem(wake + offset + NW, NW)
        looking = jnp.concatenate([targets_ref[...], points[node_slots(block), :]], axis=0)

        def run(step, gained):
            distance, moment, factors = load_source(block, pl.multiple_of(step * CHUNK, CHUNK))
            columns = source_columns(moment, factors)
            columns = jnp.concatenate(columns + [jnp.zeros_like(moment)], axis=0).astype(BF)
            for cut in range(0, CHUNK, 256):
                root = lax.rsqrt(
                    jnp.dot(looking, distance[:, cut : cut + 256], preferred_element_type=F32)
                )
                second_power = root * root
                third = second_power * root
                fifth = third[0:256] * second_power[0:256]
                high, low = split_two(fifth)
                high_node, low_node = split_two(third[256:384])
                added = dot_nt(
                    jnp.concatenate([high, low, high_node, low_node], axis=0), columns[:, cut : cut + 256]
                )
                gained = added if gained is None else gained + added
            return gained

        gained = None
        for step in range(PB // CHUNK):
            gained = run(step, gained)
        total[...] += gained[0:256] + gained[256:512]
        sums = gained[512:640] + gained[640:768]
        node_total[node_slots(block), :] = sums[:, 0:8] + sums[:, 40:48] + sums[:, 80:88]

    def far(offset):
        block = lax.rem(wake + offset + NW, NW)
        looking = points[node_slots(block), :]
        gained = None
        for step in range(PB // CHUNK):
            distance, moment, _ = load_source(block, pl.multiple_of(step * CHUNK, CHUNK))
            columns = source_columns(moment, [])
            columns = jnp.concatenate(columns + [jnp.zeros_like(moment)], axis=0).astype(BF)
            root = lax.rsqrt(jnp.dot(looking, distance, preferred_element_type=F32))
            high, low = split_two(root * root * root)
            added = dot_nt(jnp.concatenate([high, low], axis=0), columns)
            gained = added if gained is None else gained + added
        sums = gained[0:128] + gained[128:256]
        node_total[node_slots(block), :] = sums[:, 0:8] + sums[:, 8:16] + sums[:, 16:24]

    def loop(function, start):
        def body(turn, carry):
            function(start + 2 * turn)
            return carry

        lax.fori_loop(0, NW // 4, body, 0)

    for copy in second:
        copy.wait_recv()
    third_copy = send(
        gathered.at[:, side], gathered.at[:, side], send_three, recv_three, 0, (1 - 2 * side, 0)
    )
    loop(near, -4)
    loop(far, 4)
    third_copy.wait_recv()
    loop(far, 5)
    loop(near, -3)

    answers[...] = jnp.zeros_like(answers)

    def return_nodes(part, carry):
        start = pl.multiple_of(part * 256, 256)
        slot_rows = lax.broadcasted_iota(jnp.int32, (256, 1024), 0) + part * 256
        chosen = jnp.where(slot_rows == slot, 1.0, 0.0).astype(BF)
        named = jnp.sum(jnp.where(slot_rows == slot, 1.0, 0.0), axis=1, keepdims=True) > 0.0
        gained = jnp.where(named, node_total[pl.ds(start, 256), :], 0.0)
        high, mid, low = split_three(gained)
        stacked = jnp.concatenate([high, mid, low, jnp.zeros_like(low)], axis=1).astype(BF)
        answers[...] += lax.dot_general(
            stacked, chosen, (((0,), (0,)), ((), ())), preferred_element_type=F32
        )
        return carry

    lax.fori_loop(0, 8, return_nodes, 0)
    found = answers[0:8] + answers[8:16] + answers[16:24]
    moved = cross_rows(spots, [found[c : c + 1] for c in range(3)])
    for c in range(3):
        result = (moved[c] - found[3 + c : 4 + c]) * SCALE
        even = jnp.concatenate([result[:, 128 * k : 128 * (k + 1)] for k in range(8)], axis=0)
        odd = pltpu.roll(even, 64, 1)
        own_nodes[c] = jnp.concatenate(
            [(even, odd)[r % 2][r // 2 : r // 2 + 1] for r in range(16)], axis=0
        )
    shared = [
        send(own_nodes, far_nodes.at[k], send_node, recv_node, k, peer)
        for k, peer in enumerate([(0, -1), (-1, 0), (1, 0), (-1, -1), (1, -1)])
    ]

    spin = [own[3 + c : 4 + c] for c in range(3)]
    sums = jnp.transpose(total[...])
    sums = sums[0:40] + sums[40:80] + sums[80:120]
    plain = [sums[k : k + 1] for k in range(6)]
    turned = [[sums[8 + 8 * c + k : 9 + 8 * c + k] for k in range(6)] for c in range(3)]
    heavy = [sums[32 + k : 33 + k] for k in range(6)]
    mixed = [
        weight * plain[k]
        + heavy[k]
        - 2.0 * (place[0] * turned[0][k] + place[1] * turned[1][k] + place[2] * turned[2][k])
        for k in range(6)
    ]
    live = grid * 256 + lax.broadcasted_iota(jnp.int32, (1, 256), 1) < counts[wake]
    factor = jnp.where(live, SCALE, 0.0)
    swept = cross_rows(place, mixed[0:3])
    bent_own = cross_rows(place, plain[0:3])
    along = spin[0] * place[0] + spin[1] * place[1] + spin[2] * place[2]
    pulled = [spin[0] * turned[0][k] + spin[1] * turned[1][k] + spin[2] * turned[2][k] for k in range(6)]
    bent_far = cross_rows(place, pulled[0:3])
    lifted = cross_rows(spin, mixed[0:3])
    for c in range(3):
        velocity_out[c : c + 1, :] = (swept[c] - mixed[3 + c]) * factor
        bent = along * (bent_own[c] - plain[3 + c]) - (bent_far[c] - pulled[3 + c])
        stretch_out[c : c + 1, :] = (lifted[c] - 3.0 * bent) * factor

    for copy in shared + halos:
        copy.wait()
    for copy in first + second + [third_copy]:
        copy.wait_send()


ANY = pl.BlockSpec(memory_space=pl.ANY)
SCALAR = pl.BlockSpec(memory_space=pltpu.SMEM)


def gather_and_sum(counts, place, spin, core, node_place, node_block, flow, sections):
    dma = pltpu.SemaphoreType.DMA
    return pl.pallas_call(
        gather_kernel,
        out_shape=[
            jax.ShapeDtypeStruct((3, 256), F32),
            jax.ShapeDtypeStruct((3, 256), F32),
            jax.ShapeDtypeStruct((3, 16, 128), F32),
            jax.ShapeDtypeStruct((5, 3, 16, 128), F32),
            jax.ShapeDtypeStruct((5, 8, BUFFER), F32),
            jax.ShapeDtypeStruct((5, 16, 128), F32),
            jax.ShapeDtypeStruct((5, 16, 128), F32),
            jax.ShapeDtypeStruct((8, BUFFER), jnp.int32),
            jax.ShapeDtypeStruct((16, 128), jnp.int32),
            jax.ShapeDtypeStruct((16, 128), jnp.int32),
        ],
        in_specs=[SCALAR] + [ANY] * 7,
        out_specs=[WHOLE] * 4 + [ANY] * 6,
        scratch_shapes=[
            pltpu.VMEM((NW // 2, 2, 8, PB), F32),
            pltpu.VMEM((3, 3, 256), F32),
            pltpu.VMEM((3, 1024), F32),
            pltpu.VMEM((1, 1024), jnp.int32),
            pltpu.VMEM((NW * 128, 48), BF),
            pltpu.VMEM((256, 48), BF),
            pltpu.VMEM((256, 128), F32),
            pltpu.VMEM((NW * 128, 8), F32),
            pltpu.VMEM((32, 1024), F32),
            dma((5,)),
            dma((NG - 1,)),
            dma((NG - 1,)),
            dma((NG - 1,)),
            dma((NG - 1,)),
            dma((1,)),
            dma((1,)),
            dma((16,)),
            dma((16,)),
            dma((5,)),
            dma((5,)),
        ],
        compiler_params=pltpu.CompilerParams(
            collective_id=0, has_side_effects=True, vmem_limit_bytes=40 << 20
        ),
    )(counts, place, spin, core, node_place, node_block, flow, sections)


TILES = 13
STEPS = 10
BUFFER = 16640 + 256


def sweep_kernel(
    flow, sections, viscosity, rows_halo, left_halo, right_halo, kind_rows, kind_left, kind_right,
    own_nodes, far_nodes, velocity, stretch, out, velocity_out, stretch_out,
    rows_in, kind, first, second, rates, rows_out, nodes, sem_in, sem_out,
):
    fields = 5
    wake = lax.axis_index("wake")
    grid = lax.axis_index("grid")
    own_rows, halo_rows = pl.ds(0, 16), pl.ds(16, 8)
    middle, before, after = pl.ds(256, 16384), pl.ds(128, 128), pl.ds(16640, 128)
    kinds = [
        pltpu.make_async_copy(source, target, sem_in.at[4 * fields + k])
        for k, (source, target) in enumerate(
            [
                (sections, kind.at[own_rows, middle]),
                (kind_rows, kind.at[halo_rows, :]),
                (kind_left, kind.at[own_rows, before]),
                (kind_right, kind.at[own_rows, after]),
            ]
        )
    ]
    incoming = [
        [
            pltpu.make_async_copy(source, target, sem_in.at[4 * f + k])
            for k, (source, target) in enumerate(
                [
                    (flow.at[f], rows_in.at[f, own_rows, middle]),
                    (rows_halo.at[f], rows_in.at[f, halo_rows, :]),
                    (left_halo.at[f], rows_in.at[f, own_rows, before]),
                    (right_halo.at[f], rows_in.at[f, own_rows, after]),
                ]
            )
        ]
        for f in range(fields)
    ]
    for copy in kinds + [copy for f in ORDER for copy in incoming[f]]:
        copy.start()
    velocity_out[...] = velocity[...]
    stretch_out[...] = stretch[...]

    lane = lax.broadcasted_iota(jnp.int32, (24, 128), 1)
    row = lax.broadcasted_iota(jnp.int32, (24, 128), 0)
    is_first, is_last = lane == 0, lane == 127
    inside_rows = ((row < 20) | (wake > 0)) & ((row < 16) | (row >= 20) | (wake < NW - 1))
    lane8 = lax.broadcasted_iota(jnp.int32, (8, 128), 1)
    row8 = lax.broadcasted_iota(jnp.int32, (8, 128), 0)

    for c in range(3):
        def with_next(rows, column):
            return jnp.where(lane8 == 64, jnp.broadcast_to(column, (8, 128)), rows)

        halo = jnp.where(row8 < 4, far_nodes[1, c, 0:8], far_nodes[2, c, 8:16])
        halo_next = jnp.where(row8 < 4, far_nodes[3, c, 0:8], far_nodes[4, c, 8:16])
        parts = [
            with_next(own_nodes[c, 0:8], far_nodes[0, c, 0:8, 0:1]),
            with_next(own_nodes[c, 8:16], far_nodes[0, c, 8:16, 0:1]),
            with_next(halo, halo_next[:, 0:1]),
        ]
        nodes[c] = jnp.where(inside_rows, jnp.concatenate(parts, axis=0), 0.0)

    for copy in kinds:
        copy.wait()

    tile_lanes = lambda t: pl.ds(pl.multiple_of(t * 128, 128), 128)

    outgoing = []
    for f in ORDER:
        for copy in incoming[f]:
            copy.wait()
        rows_in[f, 16:24, 256:16640] = jnp.where(
            inside_rows[16:24, 0:1], rows_in[f, 16:24, 256:16640], 0.0
        )
        for start, edge in ((128, grid == 0), (16640, grid == NG - 1)):
            keep = inside_rows & jnp.logical_not(edge)
            rows_in[f, :, start : start + 128] = jnp.where(keep, rows_in[f, :, start : start + 128], 0.0)
        if f in (1, 2, 3):
            for k in range(65):
                start = 256 + 256 * k
                column = jnp.broadcast_to(nodes[f - 1, :, k : k + 1], (24, 128))
                if k == 64:
                    column = jnp.where(grid == NG - 1, 0.0, column)
                rows_in[f, :, start : start + 128] = jnp.where(
                    is_first, column, rows_in[f, :, start : start + 128]
                )

        def sweep(load, finish):
            def body(step, carry):
                last_right, here, right, left = carry
                for k in range(TILES):
                    t = step * TILES + k + 1
                    following = load(t + 1)
                    next_right = pltpu.roll(following, 1, 1)
                    next_left = pltpu.roll(following, 127, 1)
                    across = jnp.where(is_first, last_right, right) + jnp.where(is_last, next_left, left)
                    along = pltpu.roll(here, 1, 0) + pltpu.roll(here, 23, 0)
                    finish(t, here, across + along)
                    last_right, here, right, left = right, following, next_right, next_left
                return last_right, here, right, left

            start = load(1)
            lax.fori_loop(
                0, STEPS, body, (pltpu.roll(load(0), 1, 1), start, pltpu.roll(start, 1, 1), pltpu.roll(start, 127, 1))
            )

        def finish_first(t, here, beside):
            name = kind[:, tile_lanes(t)]
            rate = jnp.where(
                name == 0, viscosity[0, f], jnp.where(name == 1, viscosity[1, f], viscosity[2, f])
            )
            keep = inside_rows & jnp.logical_not(((t == 1) & (grid == 0)) | ((t == 130) & (grid == NG - 1)))
            rate = jnp.where(keep, rate, 0.0)
            rates[:, tile_lanes(t)] = rate
            first[:, tile_lanes(t)] = here + rate * (beside - 4.0 * here)

        def finish_second(t, here, beside):
            second[:, tile_lanes(t)] = here + rates[:, tile_lanes(t)] * (beside - 4.0 * here)

        def finish_third(t, here, beside):
            rows_out[f, :, tile_lanes(t)] = (here + rates[:, tile_lanes(t)] * (beside - 4.0 * here))[0:16]

        sweep(lambda t: rows_in[f, :, tile_lanes(t)], finish_first)
        sweep(lambda t: first[:, tile_lanes(t)], finish_second)
        sweep(lambda t: second[:, tile_lanes(t)], finish_third)
        copy = pltpu.make_async_copy(rows_out.at[f, :, middle], out.at[f], sem_out.at[f])
        copy.start()
        outgoing.append(copy)
    for copy in outgoing:
        copy.wait()


ORDER = (0, 4, 1, 2, 3)


def sweep_fields(*arrays):
    dma = pltpu.SemaphoreType.DMA
    return pl.pallas_call(
        sweep_kernel,
        out_shape=[
            jax.ShapeDtypeStruct((5, 16, 16384), F32),
            jax.ShapeDtypeStruct((3, 256), F32),
            jax.ShapeDtypeStruct((3, 256), F32),
        ],
        in_specs=[ANY, ANY, SCALAR] + [ANY] * 6 + [WHOLE] * 4,
        out_specs=[ANY, WHOLE, WHOLE],
        scratch_shapes=[
            pltpu.VMEM((5, 24, BUFFER), F32),
            pltpu.VMEM((24, BUFFER), jnp.int32),
            pltpu.VMEM((24, BUFFER), F32),
            pltpu.VMEM((24, BUFFER), F32),
            pltpu.VMEM((24, BUFFER), F32),
            pltpu.VMEM((5, 16, BUFFER), F32),
            pltpu.VMEM((3, 24, 128), F32),
            dma((24,)),
            dma((5,)),
        ],
        compiler_params=pltpu.CompilerParams(vmem_limit_bytes=56 << 20),
    )(*arrays)


def on_device(
    flow,
    section_map,
    viscosity,
    particle_position,
    particle_strength,
    particle_core,
    shed_counts,
    node_position,
    node_block,
):
    (
        velocity, stretch, own_nodes, far_nodes, rows_halo, left_halo, right_halo, kind_rows, kind_left, kind_right,
    ) = gather_and_sum(
        shed_counts,
        particle_position,
        particle_strength,
        particle_core.reshape(1, 256),
        node_position,
        node_block.reshape(1, 1024),
        flow,
        section_map,
    )
    field, velocity, stretch = sweep_fields(
        flow, section_map, viscosity, rows_halo, left_halo, right_halo, kind_rows, kind_left, kind_right,
        own_nodes, far_nodes, velocity, stretch,
    )
    return (field, velocity, stretch)


def solution(mesh):
    return jax.shard_map(
        on_device,
        mesh=mesh,
        in_specs=(
            P(None, "wake", "grid"),
            P("wake", "grid"),
            P(),
            P(None, ("wake", "grid")),
            P(None, ("wake", "grid")),
            P(("wake", "grid")),
            P(),
            P(None, ("wake", "grid")),
            P(("wake", "grid"), None),
        ),
        out_specs=(P(None, "wake", "grid"), P(None, ("wake", "grid")), P(None, ("wake", "grid"))),
        check_vma=False,
    )
```

time: 872 us -> 112 us (0.13); the launches traced: 857 us -> 111 us
  other arithmetic: 422 us -> 0 us
  local copies, waits for them, and re-layouts: 277 us -> 15 us
  starting transfers between devices: 105 us -> 0 us
  Pallas kernels: 0 us -> 95 us
  waiting for transfers between devices: 27.4 us -> 0 us
  blocking collectives: 22.6 us -> 0 us
    scatter x128 -> x0, other arithmetic: 291 us -> none
    scatter x194 -> x0, local copies, waits for them, and re-layouts: 229 us -> none
    pallas_call x0 -> x2, Pallas kernels: none -> 95 us  [the longest x1 66.4 us: gather_and_sum(): pl.pallas_call(gather_kernel, out_shape=[jax.ShapeDtypeStruct((3, 256), F...]
    ppermute x20 -> x0, starting transfers between devices: 90.8 us -> none  [the longest x8 41.4 us: from_behind(): lax.ppermute(value, axis, [(i, (i + by) % count) for i in range(count)])]
    reduce_sum x17 -> x0, other arithmetic: 63.4 us -> none  [the longest x8 39.1 us: particle_rates(): jnp.sum(steep * along * curl[component], axis=1)]
    add x10 -> x0, other arithmetic: 39.6 us -> none  [the longest x3 39.5 us: on_device(): field = field + diffusion * (beside - 4.0 * field)]
    ppermute x20 -> x0, waiting for transfers between devices: 27.4 us -> none  [the longest x6 16 us: extended(): lax.ppermute(head, axis, [((i + 1) % count, i) for i in range(ends)])]
    all_gather x1 -> x0, blocking collectives: 22.6 us -> none  [on_device(): block = lax.all_gather(share, 'grid', axis=1, tiled=True)]
  transfers between devices with their start and end apart: 22 -> 0, of which waited for: 8 -> 0; matrix products, arithmetic and copies ran while one was open for 73% -> 0% of each run, Pallas kernels for 0% -> 0%
where the time goes in v2:
time: 112 us; the launch traced here: 111 us
  Pallas kernels  95 us (85%)
  local copies, waits for them, and re-layouts  15 us (13%)
    pallas_call x1, Pallas kernels, gather_and_sum(): pl.pallas_call(gather_kernel, out_shape=[jax.ShapeDtypeStruct((3, 256), F...  66.4 us
    pallas_call x1, Pallas kernels, sweep_fields(): pl.pallas_call(sweep_kernel, out_shape=[jax.ShapeDtypeStruct((5, 16, 1638...  28.6 us
    unnamed x36, local copies, waits for them, and re-layouts  15 us

profile of v2, /device:TPU:39, one launch (start us, length us, event | category | flops | bytes accessed | tf_op | source)
XLA Modules:
  0.0 110.6 jit_solution(5056653600905018954)
XLA Ops:
  0.6 0.0 copy-start
  0.6 2.5 %copy-done = f32[5,16,16384]{2,1,0:T(8,128)S(1)} copy-done((f32[5,16,16384]{2,1,0:T(8,128)S(1)}, f32[5,16,16384]{2,1,0:T(8,128)}, u32[]{:S(2)}) %copy-start) | copy-done | bytes 5242904
  3.1 0.0 copy-start.1
  3.1 1.2 %copy-done.1 = s32[16,16384]{1,0:T(8,128)S(1)} copy-done((s32[16,16384]{1,0:T(8,128)S(1)}, s32[16,16384]{1,0:T(8,128)}, u32[]{:S(2)}) %copy-start.1) | copy-done | bytes 1048600
  4.3 0.0 copy-start.8
  4.3 0.7 copy-done.8
  5.1 0.0 copy-start.11
  5.1 0.7 copy-done.11
  5.8 0.0 copy-start.12
  5.8 0.7 copy-done.12
  6.4 0.0 copy-start.13
  6.4 0.7 copy-done.13
  7.1 0.0 copy-start.16
  7.1 0.7 copy-done.16
  7.8 0.0 copy-start.17
  7.8 0.7 copy-done.17
  8.5 66.4 %shard_map.112 = (f32[3,256]{1,0:T(4,128)S(1)}, f32[3,256]{1,0:T(4,128)S(1)}, f32[3,16,128]{2,1,0:T(8,128)S(1)}, f32[5,3,16,128]{3,2,1,0:T(8,128)S(1)}, f32[5,8,...) custom-call(s32[16]{0:T(128)S(1)} %copy-done.17, ...), custom_call_target="tpu_custom_call" | custom-call | tf_op jit(solution)/shard_map/pallas_call | solution.py:362
  74.9 0.0 copy-start.2
  74.9 1.5 %copy-done.2 = f32[5,8,16896]{2,1,0:T(8,128)} copy-done((f32[5,8,16896]{2,1,0:T(8,128)}, f32[5,8,16896]{2,1,0:T(8,128)S(1)}, u32[]{:S(2)}) %copy-start.2) | copy-done | bytes 2703384
  76.4 0.0 copy-start.3
  76.4 0.8 copy-done.3
  77.2 0.0 copy-start.4
  77.2 0.7 copy-done.4
  77.8 0.0 copy-start.5
  77.8 0.6 copy-done.5
  78.5 0.0 copy-start.6
  78.5 0.6 copy-done.6
  79.1 0.0 copy-start.7
  79.1 0.6 copy-done.7
  79.7 0.0 copy-start.9
  79.7 0.6 copy-done.9
  80.3 0.0 copy-start.10
  80.3 0.6 copy-done.10
  80.9 0.0 copy-start.14
  80.9 0.6 copy-done.14
  81.4 0.0 copy-start.15
  81.4 0.6 copy-done.15
  82.0 28.6 %shard_map.113 = (f32[5,16,16384]{2,1,0:T(8,128)}, f32[3,256]{1,0:T(4,128)}, f32[3,256]{1,0:T(4,128)}) custom-call(f32[5,16,16384]{2,1,0:T(8,128)} %flow.3, s32[16,16384]{1,0:T(8,128)} %sections.3, f32[3,5]{1,0:T(4,128)} %viscosity.1, f32[5,8,16896]{2,1,0:T(8,128)} %copy-done.2, f32[5,16,128]{2,1,0:T(8,128)} %copy-done.5, f32[5,16,128]{2,1,0:T(8,128)} %copy-done.6, ...), custom_call_target="tpu_custom_call" | custom-call | tf_op jit(solution)/shard_map/pallas_call | solution.py:546
Async XLA Ops:
  0.6 2.5 %copy-start = (f32[5,16,16384]{2,1,0:T(8,128)S(1)}, f32[5,16,16384]{2,1,0:T(8,128)}, u32[]{:S(2)}) copy-start(f32[5,16,16384]{2,1,0:T(8,128)} %flow.3) | copy-start | bytes 15728644
  3.1 1.2 %copy-start.1 = (s32[16,16384]{1,0:T(8,128)S(1)}, s32[16,16384]{1,0:T(8,128)}, u32[]{:S(2)}) copy-start(s32[16,16384]{1,0:T(8,128)} %sections.3) | copy-start | bytes 3145732
  4.3 0.7 copy-start.8
  5.1 0.7 copy-start.11
  5.8 0.7 copy-start.12
  6.4 0.7 copy-start.13
  7.1 0.7 copy-start.16
  7.8 0.7 copy-start.17
  74.9 1.5 %copy-start.2 = (f32[5,8,16896]{2,1,0:T(8,128)}, f32[5,8,16896]{2,1,0:T(8,128)S(1)}, u32[]{:S(2)}) copy-start(f32[5,8,16896]{2,1,0:T(8,128)S(1)} %get-tuple-element.13.rows_halo) | copy-start | bytes 8110084
  76.4 0.8 copy-start.3
  77.2 0.7 copy-start.4
  77.8 0.6 copy-start.5
  78.5 0.6 copy-start.6
  79.1 0.6 copy-start.7
  79.7 0.6 copy-start.9
  80.3 0.6 copy-start.10
  80.9 0.6 copy-start.14
  81.4 0.6 copy-start.15

commit v3 on v2

--- a/solution.py
+++ b/solution.py
@@ -11,6 +11,7 @@
 NW = 16
 NG = 8
 CHUNK = 512
+LIMIT = 64 << 20
 BF = jnp.bfloat16
 F32 = jnp.float32
 MESH = pl.DeviceIdType.MESH
@@ -121,8 +122,8 @@
     )
     pl.semaphore_wait(barrier, len(peers))
 
-    def send(source, target, sends, recvs, slot, peer):
-        copy = pltpu.make_async_remote_copy(
+    def describe(source, target, sends, recvs, slot, peer):
+        return pltpu.make_async_remote_copy(
             src_ref=source,
             dst_ref=target,
             send_sem=sends.at[slot],
@@ -130,6 +131,9 @@
             device_id=device(*peer),
             device_id_type=MESH,
         )
+
+    def send(*arguments):
+        copy = describe(*arguments)
         copy.start()
         return copy
 
@@ -190,20 +194,27 @@
     ]
     halos = []
     for k, (peer, from_rows, from_lanes, which, to_rows, to_lanes) in enumerate(plan):
-        target = (rows_halo, left_halo, right_halo)[which]
-        halos.append(
-            send(
-                flow.at[:, from_rows, from_lanes], target.at[:, to_rows, to_lanes],
-                send_halo, recv_halo, 2 * k, peer,
-            )
-        )
-        target = (kind_rows, kind_left, kind_right)[which]
-        halos.append(
-            send(
-                sections.at[from_rows, from_lanes], target.at[to_rows, to_lanes],
-                send_halo, recv_halo, 2 * k + 1, peer,
-            )
-        )
+        for part, (source, targets) in enumerate(
+            [
+                (flow.at[:, from_rows, from_lanes], (rows_halo, left_halo, right_halo)),
+                (sections.at[from_rows, from_lanes], (kind_rows, kind_left, kind_right)),
+            ]
+        ):
+            target = targets[which].at[:, to_rows, to_lanes] if part == 0 else targets[which].at[to_rows, to_lanes]
+            halos.append((peer, describe(source, target, send_halo, recv_halo, 2 * k + part, peer)))
+
+    def within(wake_by, grid_by):
+        to_wake, to_grid = wake + wake_by, grid + grid_by
+        return (to_wake >= 0) & (to_wake < NW) & (to_grid >= 0) & (to_grid < NG)
+
+    def start_halos():
+        for peer, copy in halos:
+            pl.when(within(*peer))(copy.start)
+
+    def finish_halos():
+        for peer, copy in halos:
+            pl.when(within(*peer))(copy.wait_send)
+            pl.when(within(-peer[0], -peer[1]))(copy.wait_recv)
 
     def place_nodes(part, carry):
         start = pl.multiple_of(part * 256, 256)
@@ -229,9 +240,11 @@
         high = value.astype(BF)
         return high, (value - high.astype(F32)).astype(BF)
 
-    def near(offset):
+    def near(offset, with_nodes=True):
         block = lax.rem(wake + offset + NW, NW)
-        looking = jnp.concatenate([targets_ref[...], points[node_slots(block), :]], axis=0)
+        looking = targets_ref[...]
+        if with_nodes:
+            looking = jnp.concatenate([looking, points[node_slots(block), :]], axis=0)
 
         def run(step, gained):
             distance, moment, factors = load_source(block, pl.multiple_of(step * CHUNK, CHUNK))
@@ -244,11 +257,10 @@
                 second_power = root * root
                 third = second_power * root
                 fifth = third[0:256] * second_power[0:256]
-                high, low = split_two(fifth)
-                high_node, low_node = split_two(third[256:384])
-                added = dot_nt(
-                    jnp.concatenate([high, low, high_node, low_node], axis=0), columns[:, cut : cut + 256]
-                )
+                weights = split_two(fifth)
+                if with_nodes:
+                    weights += split_two(third[256:384])
+                added = dot_nt(jnp.concatenate(weights, axis=0), columns[:, cut : cut + 256])
                 gained = added if gained is None else gained + added
             return gained
 
@@ -256,6 +268,8 @@
         for step in range(PB // CHUNK):
             gained = run(step, gained)
         total[...] += gained[0:256] + gained[256:512]
+        if not with_nodes:
+            return
         sums = gained[512:640] + gained[640:768]
         node_total[node_slots(block), :] = sums[:, 0:8] + sums[:, 40:48] + sums[:, 80:88]
 
@@ -274,23 +288,25 @@
         sums = gained[0:128] + gained[128:256]
         node_total[node_slots(block), :] = sums[:, 0:8] + sums[:, 8:16] + sums[:, 16:24]
 
-    def loop(function, start):
+    def loop(function, offsets):
         def body(turn, carry):
-            function(start + 2 * turn)
+            function(offsets(turn))
             return carry
 
-        lax.fori_loop(0, NW // 4, body, 0)
-
+        return lambda amount: lax.fori_loop(0, amount, body, 0)
+
+    near(0)
     for copy in second:
         copy.wait_recv()
     third_copy = send(
         gathered.at[:, side], gathered.at[:, side], send_three, recv_three, 0, (1 - 2 * side, 0)
     )
-    loop(near, -4)
-    loop(far, 4)
+    start_halos()
+    loop(near, lambda turn: 2 * turn - 4 + 2 * (turn // 2))(3)
+    loop(far, lambda turn: 2 * turn + 4)(4)
     third_copy.wait_recv()
-    loop(far, 5)
-    loop(near, -3)
+    loop(far, lambda turn: 2 * turn + 1)(6)
+    loop(near, lambda turn: 2 * turn - 3)(2)
 
     answers[...] = jnp.zeros_like(answers)
 
@@ -321,6 +337,8 @@
         send(own_nodes, far_nodes.at[k], send_node, recv_node, k, peer)
         for k, peer in enumerate([(0, -1), (-1, 0), (1, 0), (-1, -1), (1, -1)])
     ]
+
+    loop(lambda offset: near(offset, False), lambda turn: 2 * turn + 1)(2)
 
     spin = [own[3 + c : 4 + c] for c in range(3)]
     sums = jnp.transpose(total[...])
@@ -347,13 +365,14 @@
         bent = along * (bent_own[c] - plain[3 + c]) - (bent_far[c] - pulled[3 + c])
         stretch_out[c : c + 1, :] = (lifted[c] - 3.0 * bent) * factor
 
-    for copy in shared + halos:
+    for copy in shared:
         copy.wait()
+    finish_halos()
     for copy in first + second + [third_copy]:
         copy.wait_send()
 
 
-ANY = pl.BlockSpec(memory_space=pl.ANY)
+ANY = pl.BlockSpec(memory_space=pltpu.HBM)
 SCALAR = pl.BlockSpec(memory_space=pltpu.SMEM)
 
 
@@ -398,13 +417,13 @@
             dma((5,)),
         ],
         compiler_params=pltpu.CompilerParams(
-            collective_id=0, has_side_effects=True, vmem_limit_bytes=40 << 20
+            collective_id=0, has_side_effects=True, vmem_limit_bytes=LIMIT
         ),
     )(counts, place, spin, core, node_place, node_block, flow, sections)
 
 
-TILES = 13
-STEPS = 10
+TILES = 130
+STEPS = 130 // TILES
 BUFFER = 16640 + 256
 
 
@@ -429,8 +448,8 @@
             ]
         )
     ]
-    incoming = [
-        [
+    def incoming(f):
+        return [
             pltpu.make_async_copy(source, target, sem_in.at[4 * f + k])
             for k, (source, target) in enumerate(
                 [
@@ -441,9 +460,11 @@
                 ]
             )
         ]
-        for f in range(fields)
-    ]
-    for copy in kinds + [copy for f in ORDER for copy in incoming[f]]:
+
+    def outgoing(f):
+        return pltpu.make_async_copy(rows_out.at[f, :, middle], out.at[f], sem_out.at[f])
+
+    for copy in kinds + incoming(0):
         copy.start()
     velocity_out[...] = velocity[...]
     stretch_out[...] = stretch[...]
@@ -473,20 +494,27 @@
 
     tile_lanes = lambda t: pl.ds(pl.multiple_of(t * 128, 128), 128)
 
-    outgoing = []
-    for f in ORDER:
-        for copy in incoming[f]:
+    def field(f, done):
+        for copy in incoming(f):
             copy.wait()
+
+        @pl.when(f + 1 < fields)
+        def _():
+            for copy in incoming(f + 1):
+                copy.start()
+
         rows_in[f, 16:24, 256:16640] = jnp.where(
             inside_rows[16:24, 0:1], rows_in[f, 16:24, 256:16640], 0.0
         )
         for start, edge in ((128, grid == 0), (16640, grid == NG - 1)):
             keep = inside_rows & jnp.logical_not(edge)
             rows_in[f, :, start : start + 128] = jnp.where(keep, rows_in[f, :, start : start + 128], 0.0)
-        if f in (1, 2, 3):
+        @pl.when((f >= 1) & (f <= 3))
+        def _():
+            given = nodes[jnp.clip(f - 1, 0, 2)]
             for k in range(65):
                 start = 256 + 256 * k
-                column = jnp.broadcast_to(nodes[f - 1, :, k : k + 1], (24, 128))
+                column = jnp.broadcast_to(given[:, k : k + 1], (24, 128))
                 if k == 64:
                     column = jnp.where(grid == NG - 1, 0.0, column)
                 rows_in[f, :, start : start + 128] = jnp.where(
@@ -531,14 +559,12 @@
         sweep(lambda t: rows_in[f, :, tile_lanes(t)], finish_first)
         sweep(lambda t: first[:, tile_lanes(t)], finish_second)
         sweep(lambda t: second[:, tile_lanes(t)], finish_third)
-        copy = pltpu.make_async_copy(rows_out.at[f, :, middle], out.at[f], sem_out.at[f])
-        copy.start()
-        outgoing.append(copy)
-    for copy in outgoing:
-        copy.wait()
-
-
-ORDER = (0, 4, 1, 2, 3)
+        outgoing(f).start()
+        return done
+
+    lax.fori_loop(0, fields, field, 0)
+    for f in range(fields):
+        outgoing(f).wait()
 
 
 def sweep_fields(*arrays):
@@ -563,7 +589,7 @@
             dma((24,)),
             dma((5,)),
         ],
-        compiler_params=pltpu.CompilerParams(vmem_limit_bytes=56 << 20),
+        compiler_params=pltpu.CompilerParams(vmem_limit_bytes=LIMIT),
     )(*arrays)
 
 

time: 112 us -> 68.8 us (0.61)
  the two profiles are of different devices: /device:TPU:39 before, /device:TPU:7 now
where the time goes in v3:
time: 68.8 us; the launch traced here: 68.6 us
  Pallas kernels  67.8 us (99%)
  between operations  0.8 us (1%)
    pallas_call x1, Pallas kernels, gather_and_sum(): pl.pallas_call(gather_kernel, out_shape=[jax.ShapeDtypeStruct((3, 256), F...  50.2 us
    pallas_call x1, Pallas kernels, sweep_fields(): pl.pallas_call(sweep_kernel, out_shape=[jax.ShapeDtypeStruct((5, 16, 1638...  17.6 us

profile of v3, /device:TPU:7, one launch (start us, length us, event | category | flops | bytes accessed | tf_op | source)
XLA Modules:
  0.0 68.6 jit_solution(2585173138694478017)
XLA Ops:
  0.6 50.2 %shard_map.112 = (f32[3,256]{1,0:T(4,128)}, f32[3,256]{1,0:T(4,128)}, f32[3,16,128]{2,1,0:T(8,128)}, f32[5,3,16,128]{3,2,1,0:T(8,128)}, f32[5,8,16896]{2,1,0:T(8...) custom-call(s32[16]{0:T(128)} %counts.1, ...), custom_call_target="tpu_custom_call" | custom-call | tf_op jit(solution)/shard_map/pallas_call | solution.py:381
  50.9 17.6 %shard_map.113 = (f32[5,16,16384]{2,1,0:T(8,128)}, f32[3,256]{1,0:T(4,128)}, f32[3,256]{1,0:T(4,128)}) custom-call(f32[5,16,16384]{2,1,0:T(8,128)} %flow.3, s32[16,16384]{1,0:T(8,128)} %sections.3, f32[3,5]{1,0:T(4,128)} %viscosity.1, f32[5,8,16896]{2,1,0:T(8,128)} %get-tuple-element.13.rows_halo, f32[5,16,128]{2,1,0:T(8,128)} %get-tuple-element.14.left_halo, ...), custom_call_target="tpu_custom_call" | custom-call | tf_op jit(solution)/shard_map/pallas_call | solution.py:572

commit v4 on v3

--- a/solution.py
+++ b/solution.py
@@ -41,26 +41,10 @@
 def target_rows(place, weight, halved):
     ones = jnp.ones_like(weight)
     none = jnp.zeros_like(weight)
-    parts = split_three(jnp.concatenate([-2.0 * row for row in place] + [none, none, weight, none, none], axis=0))
-    unit = jnp.concatenate([none] * 3 + [none if halved else ones, ones if halved else none] + [none] * 3, axis=0)
+    parts = split_three(jnp.concatenate([weight, none, none] + [-2.0 * row for row in place] + [none, none], axis=0))
+    unit = jnp.concatenate([none] * 6 + [none if halved else ones, ones if halved else none], axis=0)
     high, middle, low = parts
     return jnp.concatenate([high + unit, middle, low, high + unit, middle, high + unit], axis=0).astype(BF)
-
-
-def source_rows(rows, live):
-    place = rows[0:3]
-    square = place[0] * place[0] + place[1] * place[1] + place[2] * place[2]
-    core = rows[6] * rows[6]
-    half = square + 0.5 * core
-    ones = jnp.ones_like(square)
-    none = jnp.zeros_like(square)
-    high, middle, low = split_three(
-        jnp.concatenate(list(place) + [square + core, half, ones, none, none], axis=0)
-    )
-    distance = jnp.concatenate([high, high, high, middle, middle, low], axis=0).astype(BF)
-    spin = [jnp.where(live, rows[3 + c], 0.0) for c in range(3)]
-    moment = jnp.concatenate(spin + cross_rows(place, spin) + [none, none], axis=0)
-    return distance, moment, half
 
 
 def source_columns(moment, factors):
@@ -69,8 +53,8 @@
     return columns
 
 
-def centred(rows):
-    return [rows[c : c + 1] - 0.5 for c in range(3)]
+def centred(rows, centre):
+    return [rows[c : c + 1] - centre[c][:, 0 : rows.shape[1]] for c in range(3)]
 
 
 def square_sum(place):
@@ -81,7 +65,7 @@
     counts, place_in, spin_in, core_in, node_place_in, node_block_in, flow, sections,
     velocity_out, stretch_out, own_nodes, far_nodes, rows_halo, left_halo, right_halo,
     kind_rows, kind_left, kind_right,
-    gathered, share, node_place, node_block, points, targets_ref, total, node_total, answers,
+    gathered, share, node_place, node_block, points, targets_ref, total, node_total,
     sem_in, send_one, recv_one, send_two, recv_two, send_three, recv_three,
     send_halo, recv_halo, send_node, recv_node,
 ):
@@ -117,8 +101,10 @@
         pl.semaphore_signal(barrier, inc=1, device_id=device(*peer), device_id_type=MESH)
     for load in loads:
         load.wait()
+    own_live = grid * 256 + lax.broadcasted_iota(jnp.int32, (1, 256), 1) < counts[wake]
+    squared_core = share[2, 0:1] * share[2, 0:1]
     mine[...] = jnp.concatenate(
-        [share[0], share[1], share[2, 0:1], jnp.zeros((1, 256), F32)], axis=0
+        [jnp.where(own_live, share[1], 0.0), share[0], squared_core, 0.5 * squared_core], axis=0
     )
     pl.semaphore_wait(barrier, len(peers))
 
@@ -137,10 +123,15 @@
         copy.start()
         return copy
 
+    own = mine[...]
+    centre = [
+        jnp.broadcast_to(jnp.sum(own[3 + c : 4 + c], axis=1, keepdims=True) * (1.0 / 256.0), (1, 1024))
+        for c in range(3)
+    ]
     first = [send(mine, mine, send_one, recv_one, turn - 1, (0, turn)) for turn in range(1, NG)]
 
     names = node_block[...]
-    spots = centred(node_place)
+    spots = centred(node_place, centre)
     rows = target_rows(spots, square_sum(spots), False)
     members = jnp.where(lax.broadcasted_iota(jnp.int32, (NW, 1024), 0) == names, 1.0, 0.0)
     triangle = jnp.where(
@@ -158,10 +149,10 @@
         before = before + part[:, 127:128]
     rank = jnp.sum(members * jnp.concatenate(ranks, axis=1), axis=0, keepdims=True) - 1.0
     slot = names * 128 + rank.astype(jnp.int32)
-
-    own = mine[...]
-    place = centred(own)
-    weight = square_sum(place) + 0.5 * own[6:7] * own[6:7]
+    slot_eight = lax.broadcasted_iota(jnp.int32, (128, 8), 0).astype(F32)
+
+    place = centred(own[3:6], centre)
+    weight = square_sum(place) + own[7:8]
     identity = jnp.where(
         lax.broadcasted_iota(jnp.int32, (256, 256), 0) == lax.broadcasted_iota(jnp.int32, (256, 256), 1),
         1.0,
@@ -216,22 +207,34 @@
             pl.when(within(*peer))(copy.wait_send)
             pl.when(within(-peer[0], -peer[1]))(copy.wait_recv)
 
-    def place_nodes(part, carry):
-        start = pl.multiple_of(part * 256, 256)
+    for part in range(8):
         chosen = jnp.where(
             lax.broadcasted_iota(jnp.int32, (256, 1024), 0) + part * 256 == slot, 1.0, 0.0
         ).astype(BF)
-        points[pl.ds(start, 256), :] = dot_nt(chosen, rows).astype(BF)
-        return carry
-
-    lax.fori_loop(0, 8, place_nodes, 0)
+        points[256 * part : 256 * (part + 1), :] = dot_nt(chosen, rows).astype(BF)
+
+    line = lax.broadcasted_iota(jnp.int32, (8, CHUNK), 0)
+    is_place = (line >= 3) & (line < 6)
+    shift = jnp.zeros((8, CHUNK), F32)
+    for c in range(3):
+        shift = jnp.where(line == 3 + c, jnp.broadcast_to(centre[c][:, 0:CHUNK], (8, CHUNK)), shift)
 
     def load_source(block, start):
-        tile = gathered[block // 2, lax.rem(block, 2), :, pl.ds(start, CHUNK)]
-        live = start + lax.broadcasted_iota(jnp.int32, (1, CHUNK), 1) < counts[block]
-        source = centred(tile) + [tile[c : c + 1] for c in range(3, 7)]
-        distance, moment, half = source_rows(source, live)
-        return distance, moment, source[0:3] + [half]
+        tile = gathered[block // 2, lax.rem(block, 2), :, pl.ds(start, CHUNK)] - shift
+        summed = jnp.where(is_place, tile * tile, 0.0)
+        for step in (4, 2, 1):
+            summed = summed + pltpu.roll(summed, step, 0)
+        full = tile + jnp.where(line >= 6, summed, 0.0)
+        high, middle, low = split_three(jnp.where(line == 0, 1.0, full))
+        distance = jnp.concatenate([high, high, high, middle, middle, low], axis=0).astype(BF)
+        down_one, down_two = pltpu.roll(tile, 1, 0), pltpu.roll(tile, 2, 0)
+        place_next = jnp.where(line == 5, down_two, pltpu.roll(tile, 7, 0))
+        place_last = jnp.where(line == 3, pltpu.roll(tile, 6, 0), down_one)
+        spin_next = jnp.where(line == 5, pltpu.roll(tile, 5, 0), down_two)
+        spin_last = jnp.where(line == 3, down_one, pltpu.roll(tile, 4, 0))
+        crossed = place_next * spin_last - place_last * spin_next
+        moment = jnp.where(line < 3, tile, jnp.where(line < 6, crossed, 0.0))
+        return distance, moment, [full[k : k + 1] for k in (3, 4, 5, 7)]
 
     def node_slots(block):
         return pl.ds(pl.multiple_of(block * 128, 128), 128)
@@ -303,27 +306,30 @@
     )
     start_halos()
     loop(near, lambda turn: 2 * turn - 4 + 2 * (turn // 2))(3)
-    loop(far, lambda turn: 2 * turn + 4)(4)
+    loop(lambda offset: [far(offset + 2 * k) for k in range(4)], lambda turn: 4 + turn)(1)
     third_copy.wait_recv()
-    loop(far, lambda turn: 2 * turn + 1)(6)
+    loop(lambda offset: [far(offset + 2 * k) for k in range(3)], lambda turn: 6 * turn + 1)(2)
     loop(near, lambda turn: 2 * turn - 3)(2)
 
-    answers[...] = jnp.zeros_like(answers)
-
-    def return_nodes(part, carry):
-        start = pl.multiple_of(part * 256, 256)
+    answers = None
+    for part in range(8):
         slot_rows = lax.broadcasted_iota(jnp.int32, (256, 1024), 0) + part * 256
         chosen = jnp.where(slot_rows == slot, 1.0, 0.0).astype(BF)
-        named = jnp.sum(jnp.where(slot_rows == slot, 1.0, 0.0), axis=1, keepdims=True) > 0.0
-        gained = jnp.where(named, node_total[pl.ds(start, 256), :], 0.0)
+        gained = jnp.concatenate(
+            [
+                jnp.where(
+                    slot_eight < before[block : block + 1],
+                    node_total[128 * block : 128 * (block + 1), :],
+                    0.0,
+                )
+                for block in (2 * part, 2 * part + 1)
+            ],
+            axis=0,
+        )
         high, mid, low = split_three(gained)
         stacked = jnp.concatenate([high, mid, low, jnp.zeros_like(low)], axis=1).astype(BF)
-        answers[...] += lax.dot_general(
-            stacked, chosen, (((0,), (0,)), ((), ())), preferred_element_type=F32
-        )
-        return carry
-
-    lax.fori_loop(0, 8, return_nodes, 0)
+        added = lax.dot_general(stacked, chosen, (((0,), (0,)), ((), ())), preferred_element_type=F32)
+        answers = added if answers is None else answers + added
     found = answers[0:8] + answers[8:16] + answers[16:24]
     moved = cross_rows(spots, [found[c : c + 1] for c in range(3)])
     for c in range(3):
@@ -340,7 +346,7 @@
 
     loop(lambda offset: near(offset, False), lambda turn: 2 * turn + 1)(2)
 
-    spin = [own[3 + c : 4 + c] for c in range(3)]
+    spin = [own[c : c + 1] for c in range(3)]
     sums = jnp.transpose(total[...])
     sums = sums[0:40] + sums[40:80] + sums[80:120]
     plain = [sums[k : k + 1] for k in range(6)]
@@ -403,7 +409,6 @@
             pltpu.VMEM((256, 48), BF),
             pltpu.VMEM((256, 128), F32),
             pltpu.VMEM((NW * 128, 8), F32),
-            pltpu.VMEM((32, 1024), F32),
             dma((5,)),
             dma((NG - 1,)),
             dma((NG - 1,)),

time: 68.8 us -> 62.8 us (0.913)
  Pallas kernels: 67.8 us -> 61.8 us
    pallas_call x1, Pallas kernels: 50.2 us -> 44.2 us  [gather_and_sum(): pl.pallas_call(gather_kernel, out_shape=[jax.ShapeDtypeStruct((3, 256), F...]
where the time goes in v4:
time: 62.8 us; the launch traced here: 62.6 us
  Pallas kernels  61.8 us (98%)
  between operations  0.82 us (1%)
    pallas_call x1, Pallas kernels, gather_and_sum(): pl.pallas_call(gather_kernel, out_shape=[jax.ShapeDtypeStruct((3, 256), F...  44.2 us
    pallas_call x1, Pallas kernels, sweep_fields(): pl.pallas_call(sweep_kernel, out_shape=[jax.ShapeDtypeStruct((5, 16, 1638...  17.6 us

profile of v4, /device:TPU:7, one launch (start us, length us, event | category | flops | bytes accessed | tf_op | source)
XLA Modules:
  0.0 62.6 jit_solution(3375746349109267842)
XLA Ops:
  0.6 44.2 %shard_map.112 = (f32[3,256]{1,0:T(4,128)}, f32[3,256]{1,0:T(4,128)}, f32[3,16,128]{2,1,0:T(8,128)}, f32[5,3,16,128]{3,2,1,0:T(8,128)}, f32[5,8,16896]{2,1,0:T(8...) custom-call(s32[16]{0:T(128)} %counts.1, ...), custom_call_target="tpu_custom_call" | custom-call | tf_op jit(solution)/shard_map/pallas_call | solution.py:387
  44.8 17.6 %shard_map.113 = (f32[5,16,16384]{2,1,0:T(8,128)}, f32[3,256]{1,0:T(4,128)}, f32[3,256]{1,0:T(4,128)}) custom-call(f32[5,16,16384]{2,1,0:T(8,128)} %flow.3, s32[16,16384]{1,0:T(8,128)} %sections.3, f32[3,5]{1,0:T(4,128)} %viscosity.1, f32[5,8,16896]{2,1,0:T(8,128)} %get-tuple-element.13.rows_halo, f32[5,16,128]{2,1,0:T(8,128)} %get-tuple-element.14.left_halo, ...), custom_call_target="tpu_custom_call" | custom-call | tf_op jit(solution)/shard_map/pallas_call | solution.py:577

commit v5 on v4

--- a/solution.py
+++ b/solution.py
@@ -165,7 +165,7 @@
         copy.wait_recv()
     block_here = gathered.at[pair, side]
     second = [
-        send(block_here, block_here, send_two, recv_two, turn - 1, (2 * turn, 0)) for turn in range(1, NG)
+        send(block_here, block_here, send_two, recv_two, turn - 1, (2 * turn, 0)) for turn in (1, 2, 7, 3, 4, 5, 6)
     ]
 
     top, bottom = pl.ds(0, 3), pl.ds(13, 3)
@@ -253,9 +253,9 @@
             distance, moment, factors = load_source(block, pl.multiple_of(step * CHUNK, CHUNK))
             columns = source_columns(moment, factors)
             columns = jnp.concatenate(columns + [jnp.zeros_like(moment)], axis=0).astype(BF)
-            for cut in range(0, CHUNK, 256):
+            for cut in range(0, CHUNK, CHUNK):
                 root = lax.rsqrt(
-                    jnp.dot(looking, distance[:, cut : cut + 256], preferred_element_type=F32)
+                    jnp.dot(looking, distance[:, cut : cut + CHUNK], preferred_element_type=F32)
                 )
                 second_power = root * root
                 third = second_power * root
@@ -263,7 +263,7 @@
                 weights = split_two(fifth)
                 if with_nodes:
                     weights += split_two(third[256:384])
-                added = dot_nt(jnp.concatenate(weights, axis=0), columns[:, cut : cut + 256])
+                added = dot_nt(jnp.concatenate(weights, axis=0), columns[:, cut : cut + CHUNK])
                 gained = added if gained is None else gained + added
             return gained
 
@@ -298,14 +298,19 @@
 
         return lambda amount: lax.fori_loop(0, amount, body, 0)
 
-    near(0)
-    for copy in second:
+    def near_even(turn):
+        for k in range(2):
+            pl.when(turn == k + 1)(second[k].wait_recv)
+        near(-2 * turn)
+
+    loop(near_even, lambda turn: turn)(3)
+    for copy in second[2:]:
         copy.wait_recv()
     third_copy = send(
         gathered.at[:, side], gathered.at[:, side], send_three, recv_three, 0, (1 - 2 * side, 0)
     )
     start_halos()
-    loop(near, lambda turn: 2 * turn - 4 + 2 * (turn // 2))(3)
+    near(2)
     loop(lambda offset: [far(offset + 2 * k) for k in range(4)], lambda turn: 4 + turn)(1)
     third_copy.wait_recv()
     loop(lambda offset: [far(offset + 2 * k) for k in range(3)], lambda turn: 6 * turn + 1)(2)
@@ -428,7 +433,6 @@
 
 
 TILES = 130
-STEPS = 130 // TILES
 BUFFER = 16640 + 256
 
 
@@ -466,8 +470,12 @@
             )
         ]
 
-    def outgoing(f):
-        return pltpu.make_async_copy(rows_out.at[f, :, middle], out.at[f], sem_out.at[f])
+    def outgoing(f, half):
+        return pltpu.make_async_copy(
+            rows_out.at[f, :, pl.ds(256 + 8192 * half, 8192)],
+            out.at[f, :, pl.ds(8192 * half, 8192)],
+            sem_out.at[2 * f + half],
+        )
 
     for copy in kinds + incoming(0):
         copy.start()
@@ -497,7 +505,7 @@
     for copy in kinds:
         copy.wait()
 
-    tile_lanes = lambda t: pl.ds(pl.multiple_of(t * 128, 128), 128)
+    tile_lanes = lambda t: pl.ds(t * 128, 128)
 
     def field(f, done):
         for copy in incoming(f):
@@ -527,30 +535,27 @@
                 )
 
         def sweep(load, finish):
-            def body(step, carry):
-                last_right, here, right, left = carry
-                for k in range(TILES):
-                    t = step * TILES + k + 1
-                    following = load(t + 1)
-                    next_right = pltpu.roll(following, 1, 1)
-                    next_left = pltpu.roll(following, 127, 1)
-                    across = jnp.where(is_first, last_right, right) + jnp.where(is_last, next_left, left)
-                    along = pltpu.roll(here, 1, 0) + pltpu.roll(here, 23, 0)
-                    finish(t, here, across + along)
-                    last_right, here, right, left = right, following, next_right, next_left
-                return last_right, here, right, left
-
-            start = load(1)
-            lax.fori_loop(
-                0, STEPS, body, (pltpu.roll(load(0), 1, 1), start, pltpu.roll(start, 1, 1), pltpu.roll(start, 127, 1))
-            )
+            here = load(1)
+            last_right, right, left = pltpu.roll(load(0), 1, 1), pltpu.roll(here, 1, 1), pltpu.roll(here, 127, 1)
+            for t in range(1, TILES + 1):
+                following = load(t + 1)
+                next_right = pltpu.roll(following, 1, 1)
+                next_left = pltpu.roll(following, 127, 1)
+                across = jnp.where(is_first, last_right, right) + jnp.where(is_last, next_left, left)
+                along = pltpu.roll(here, 1, 0) + pltpu.roll(here, 23, 0)
+                finish(t, here, across + along)
+                last_right, here, right, left = right, following, next_right, next_left
 
         def finish_first(t, here, beside):
             name = kind[:, tile_lanes(t)]
             rate = jnp.where(
                 name == 0, viscosity[0, f], jnp.where(name == 1, viscosity[1, f], viscosity[2, f])
             )
-            keep = inside_rows & jnp.logical_not(((t == 1) & (grid == 0)) | ((t == 130) & (grid == NG - 1)))
+            keep = inside_rows
+            if t == 1:
+                keep = keep & (grid > 0)
+            if t == TILES:
+                keep = keep & (grid < NG - 1)
             rate = jnp.where(keep, rate, 0.0)
             rates[:, tile_lanes(t)] = rate
             first[:, tile_lanes(t)] = here + rate * (beside - 4.0 * here)
@@ -560,16 +565,19 @@
 
         def finish_third(t, here, beside):
             rows_out[f, :, tile_lanes(t)] = (here + rates[:, tile_lanes(t)] * (beside - 4.0 * here))[0:16]
+            if t == 65:
+                outgoing(f, 0).start()
 
         sweep(lambda t: rows_in[f, :, tile_lanes(t)], finish_first)
         sweep(lambda t: first[:, tile_lanes(t)], finish_second)
         sweep(lambda t: second[:, tile_lanes(t)], finish_third)
-        outgoing(f).start()
+        outgoing(f, 1).start()
         return done
 
     lax.fori_loop(0, fields, field, 0)
     for f in range(fields):
-        outgoing(f).wait()
+        outgoing(f, 0).wait()
+        outgoing(f, 1).wait()
 
 
 def sweep_fields(*arrays):
@@ -592,7 +600,7 @@
             pltpu.VMEM((5, 16, BUFFER), F32),
             pltpu.VMEM((3, 24, 128), F32),
             dma((24,)),
-            dma((5,)),
+            dma((10,)),
         ],
         compiler_params=pltpu.CompilerParams(vmem_limit_bytes=LIMIT),
     )(*arrays)

time: 62.8 us -> 60 us (0.955)
  the two profiles are of different devices: /device:TPU:7 before, /device:TPU:39 now
where the time goes in v5:
time: 60 us; the launch traced here: 59.8 us
  Pallas kernels  59 us (98%)
  between operations  0.8 us (1%)
    pallas_call x1, Pallas kernels, gather_and_sum(): pl.pallas_call(gather_kernel, out_shape=[jax.ShapeDtypeStruct((3, 256), F...  41.6 us
    pallas_call x1, Pallas kernels, sweep_fields(): pl.pallas_call(sweep_kernel, out_shape=[jax.ShapeDtypeStruct((5, 16, 1638...  17.4 us

profile of v5, /device:TPU:39, one launch (start us, length us, event | category | flops | bytes accessed | tf_op | source)
XLA Modules:
  0.0 59.8 jit_solution(11764080749498351811)
XLA Ops:
  0.6 41.6 %shard_map.112 = (f32[3,256]{1,0:T(4,128)}, f32[3,256]{1,0:T(4,128)}, f32[3,16,128]{2,1,0:T(8,128)}, f32[5,3,16,128]{3,2,1,0:T(8,128)}, f32[5,8,16896]{2,1,0:T(8...) custom-call(s32[16]{0:T(128)} %counts.1, ...), custom_call_target="tpu_custom_call" | custom-call | tf_op jit(solution)/shard_map/pallas_call | solution.py:392
  42.2 17.4 %shard_map.113 = (f32[5,16,16384]{2,1,0:T(8,128)}, f32[3,256]{1,0:T(4,128)}, f32[3,256]{1,0:T(4,128)}) custom-call(f32[5,16,16384]{2,1,0:T(8,128)} %flow.3, s32[16,16384]{1,0:T(8,128)} %sections.3, f32[3,5]{1,0:T(4,128)} %viscosity.1, f32[5,8,16896]{2,1,0:T(8,128)} %get-tuple-element.13.rows_halo, f32[5,16,128]{2,1,0:T(8,128)} %get-tuple-element.14.left_halo, ...), custom_call_target="tpu_custom_call" | custom-call | tf_op jit(solution)/shard_map/pallas_call | solution.py:585

commit v6 on v5

--- a/solution.py
+++ b/solution.py
@@ -63,11 +63,11 @@
 
 def gather_kernel(
     counts, place_in, spin_in, core_in, node_place_in, node_block_in, flow, sections,
-    velocity_out, stretch_out, own_nodes, far_nodes, rows_halo, left_halo, right_halo,
+    velocity_to, stretch_to, own_nodes_to, far_nodes, rows_halo, left_halo, right_halo,
     kind_rows, kind_left, kind_right,
-    gathered, share, node_place, node_block, points, targets_ref, total, node_total,
+    velocity_out, stretch_out, own_nodes, gathered, share, node_place, node_block, points, targets_ref, total, node_total,
     sem_in, send_one, recv_one, send_two, recv_two, send_three, recv_three,
-    send_halo, recv_halo, send_node, recv_node,
+    send_halo, recv_halo, send_node, recv_node, sem_out,
 ):
     wake = lax.axis_index("wake")
     grid = lax.axis_index("grid")
@@ -349,6 +349,13 @@
         for k, peer in enumerate([(0, -1), (-1, 0), (1, 0), (-1, -1), (1, -1)])
     ]
 
+    results = [
+        pltpu.make_async_copy(source, target, sem_out.at[k])
+        for k, (source, target) in enumerate(
+            [(own_nodes, own_nodes_to), (velocity_out, velocity_to), (stretch_out, stretch_to)]
+        )
+    ]
+    results[0].start()
     loop(lambda offset: near(offset, False), lambda turn: 2 * turn + 1)(2)
 
     spin = [own[c : c + 1] for c in range(3)]
@@ -376,9 +383,13 @@
         bent = along * (bent_own[c] - plain[3 + c]) - (bent_far[c] - pulled[3 + c])
         stretch_out[c : c + 1, :] = (lifted[c] - 3.0 * bent) * factor
 
+    results[1].start()
+    results[2].start()
     for copy in shared:
         copy.wait()
     finish_halos()
+    for copy in results:
+        copy.wait()
     for copy in first + second + [third_copy]:
         copy.wait_send()
 
@@ -404,8 +415,11 @@
             jax.ShapeDtypeStruct((16, 128), jnp.int32),
         ],
         in_specs=[SCALAR] + [ANY] * 7,
-        out_specs=[WHOLE] * 4 + [ANY] * 6,
+        out_specs=[ANY] * 10,
         scratch_shapes=[
+            pltpu.VMEM((3, 256), F32),
+            pltpu.VMEM((3, 256), F32),
+            pltpu.VMEM((3, 16, 128), F32),
             pltpu.VMEM((NW // 2, 2, 8, PB), F32),
             pltpu.VMEM((3, 3, 256), F32),
             pltpu.VMEM((3, 1024), F32),
@@ -425,6 +439,7 @@
             dma((16,)),
             dma((5,)),
             dma((5,)),
+            dma((3,)),
         ],
         compiler_params=pltpu.CompilerParams(
             collective_id=0, has_side_effects=True, vmem_limit_bytes=LIMIT
@@ -438,8 +453,8 @@
 
 def sweep_kernel(
     flow, sections, viscosity, rows_halo, left_halo, right_halo, kind_rows, kind_left, kind_right,
-    own_nodes, far_nodes, velocity, stretch, out, velocity_out, stretch_out,
-    rows_in, kind, first, second, rates, rows_out, nodes, sem_in, sem_out,
+    own_nodes_in, far_nodes_in, velocity, stretch, out, velocity_out, stretch_out,
+    own_nodes, far_nodes, rows_in, kind, first, second, rates, rows_out, nodes, sem_in, sem_out, sem_small,
 ):
     fields = 5
     wake = lax.axis_index("wake")
@@ -479,8 +494,21 @@
 
     for copy in kinds + incoming(0):
         copy.start()
-    velocity_out[...] = velocity[...]
-    stretch_out[...] = stretch[...]
+    small = [
+        pltpu.make_async_copy(source, target, sem_small.at[k])
+        for k, (source, target) in enumerate(
+            [
+                (own_nodes_in, own_nodes),
+                (far_nodes_in, far_nodes),
+                (velocity, velocity_out),
+                (stretch, stretch_out),
+            ]
+        )
+    ]
+    for copy in small:
+        copy.start()
+    for copy in small[0:2]:
+        copy.wait()
 
     lane = lax.broadcasted_iota(jnp.int32, (24, 128), 1)
     row = lax.broadcasted_iota(jnp.int32, (24, 128), 0)
@@ -578,6 +606,8 @@
     for f in range(fields):
         outgoing(f, 0).wait()
         outgoing(f, 1).wait()
+    for copy in small[2:4]:
+        copy.wait()
 
 
 def sweep_fields(*arrays):
@@ -589,9 +619,11 @@
             jax.ShapeDtypeStruct((3, 256), F32),
             jax.ShapeDtypeStruct((3, 256), F32),
         ],
-        in_specs=[ANY, ANY, SCALAR] + [ANY] * 6 + [WHOLE] * 4,
-        out_specs=[ANY, WHOLE, WHOLE],
+        in_specs=[ANY, ANY, SCALAR] + [ANY] * 10,
+        out_specs=[ANY] * 3,
         scratch_shapes=[
+            pltpu.VMEM((3, 16, 128), F32),
+            pltpu.VMEM((5, 3, 16, 128), F32),
             pltpu.VMEM((5, 24, BUFFER), F32),
             pltpu.VMEM((24, BUFFER), jnp.int32),
             pltpu.VMEM((24, BUFFER), F32),
@@ -601,6 +633,7 @@
             pltpu.VMEM((3, 24, 128), F32),
             dma((24,)),
             dma((10,)),
+            dma((4,)),
         ],
         compiler_params=pltpu.CompilerParams(vmem_limit_bytes=LIMIT),
     )(*arrays)

time: 60 us -> 59 us (0.983)
  Pallas kernels: 59 us -> 58 us
where the time goes in v6:
time: 59 us; the launch traced here: 58.8 us
  Pallas kernels  58 us (98%)
  between operations  0.8 us (1%)
    pallas_call x1, Pallas kernels, gather_and_sum(): pl.pallas_call(gather_kernel, out_shape=[jax.ShapeDtypeStruct((3, 256), F...  41 us
    pallas_call x1, Pallas kernels, sweep_fields(): pl.pallas_call(sweep_kernel, out_shape=[jax.ShapeDtypeStruct((5, 16, 1638...  17 us

profile of v6, /device:TPU:39, one launch (start us, length us, event | category | flops | bytes accessed | tf_op | source)
XLA Modules:
  0.0 58.8 jit_solution(11495588877623599103)
XLA Ops:
  0.6 41.0 %shard_map.112 = (f32[3,256]{1,0:T(4,128)}, f32[3,256]{1,0:T(4,128)}, f32[3,16,128]{2,1,0:T(8,128)}, f32[5,3,16,128]{3,2,1,0:T(8,128)}, f32[5,8,16896]{2,1,0:T(8...) custom-call(s32[16]{0:T(128)} %counts.1, ...), custom_call_target="tpu_custom_call" | custom-call | tf_op jit(solution)/shard_map/pallas_call | solution.py:403
  41.7 17.0 %shard_map.113 = (f32[5,16,16384]{2,1,0:T(8,128)}, f32[3,256]{1,0:T(4,128)}, f32[3,256]{1,0:T(4,128)}) custom-call(f32[5,16,16384]{2,1,0:T(8,128)} %flow.3, s32[16,16384]{1,0:T(8,128)} %sections.3, f32[3,5]{1,0:T(4,128)} %viscosity.1, f32[5,8,16896]{2,1,0:T(8,128)} %get-tuple-element.13.rows_halo, f32[5,16,128]{2,1,0:T(8,128)} %get-tuple-element.14.left_halo, ...), custom_call_target="tpu_custom_call" | custom-call | tf_op jit(solution)/shard_map/pallas_call | solution.py:615

commit v7 on v6

--- a/solution.py
+++ b/solution.py
@@ -313,8 +313,8 @@
     near(2)
     loop(lambda offset: [far(offset + 2 * k) for k in range(4)], lambda turn: 4 + turn)(1)
     third_copy.wait_recv()
-    loop(lambda offset: [far(offset + 2 * k) for k in range(3)], lambda turn: 6 * turn + 1)(2)
-    loop(near, lambda turn: 2 * turn - 3)(2)
+    loop(lambda offset: [far(offset + 2 * k) for k in range(7)], lambda turn: turn - 1)(1)
+    near(-3)
 
     answers = None
     for part in range(8):
@@ -356,7 +356,7 @@
         )
     ]
     results[0].start()
-    loop(lambda offset: near(offset, False), lambda turn: 2 * turn + 1)(2)
+    loop(lambda offset: near(offset, False), lambda turn: 2 * turn - 1)(3)
 
     spin = [own[c : c + 1] for c in range(3)]
     sums = jnp.transpose(total[...])
@@ -579,12 +579,11 @@
             rate = jnp.where(
                 name == 0, viscosity[0, f], jnp.where(name == 1, viscosity[1, f], viscosity[2, f])
             )
-            keep = inside_rows
             if t == 1:
-                keep = keep & (grid > 0)
+                rate = jnp.where(grid > 0, rate, 0.0)
             if t == TILES:
-                keep = keep & (grid < NG - 1)
-            rate = jnp.where(keep, rate, 0.0)
+                rate = jnp.where(grid < NG - 1, rate, 0.0)
+            rate = jnp.concatenate([rate[0:16], jnp.where(inside_rows[16:24], rate[16:24], 0.0)], axis=0)
             rates[:, tile_lanes(t)] = rate
             first[:, tile_lanes(t)] = here + rate * (beside - 4.0 * here)
 

time: 59 us -> 58.8 us (level)
  no operation moved by 1% of the time
where the time goes in v7:
time: 58.8 us; the launch traced here: 58.6 us
  Pallas kernels  57.8 us (98%)
  between operations  0.8 us (1%)
    pallas_call x1, Pallas kernels, gather_and_sum(): pl.pallas_call(gather_kernel, out_shape=[jax.ShapeDtypeStruct((3, 256), F...  41 us
    pallas_call x1, Pallas kernels, sweep_fields(): pl.pallas_call(sweep_kernel, out_shape=[jax.ShapeDtypeStruct((5, 16, 1638...  16.8 us

profile of v7, /device:TPU:39, one launch (start us, length us, event | category | flops | bytes accessed | tf_op | source)
XLA Modules:
  0.0 58.6 jit_solution(11703060680450024573)
XLA Ops:
  0.6 41.0 %shard_map.112 = (f32[3,256]{1,0:T(4,128)}, f32[3,256]{1,0:T(4,128)}, f32[3,16,128]{2,1,0:T(8,128)}, f32[5,3,16,128]{3,2,1,0:T(8,128)}, f32[5,8,16896]{2,1,0:T(8...) custom-call(s32[16]{0:T(128)} %counts.1, ...), custom_call_target="tpu_custom_call" | custom-call | tf_op jit(solution)/shard_map/pallas_call | solution.py:403
  41.7 16.8 %shard_map.113 = (f32[5,16,16384]{2,1,0:T(8,128)}, f32[3,256]{1,0:T(4,128)}, f32[3,256]{1,0:T(4,128)}) custom-call(f32[5,16,16384]{2,1,0:T(8,128)} %flow.3, s32[16,16384]{1,0:T(8,128)} %sections.3, f32[3,5]{1,0:T(4,128)} %viscosity.1, f32[5,8,16896]{2,1,0:T(8,128)} %get-tuple-element.13.rows_halo, f32[5,16,128]{2,1,0:T(8,128)} %get-tuple-element.14.left_halo, ...), custom_call_target="tpu_custom_call" | custom-call | tf_op jit(solution)/shard_map/pallas_call | solution.py:614

commit v8 on v7

--- a/solution.py
+++ b/solution.py
@@ -10,7 +10,7 @@
 PB = 2048
 NW = 16
 NG = 8
-CHUNK = 512
+CHUNK = 1024
 LIMIT = 64 << 20
 BF = jnp.bfloat16
 F32 = jnp.float32

time: 58.8 us -> 57.9 us (0.985)
  Pallas kernels: 57.8 us -> 56.8 us
    pallas_call x1, Pallas kernels: 41 us -> 40 us  [gather_and_sum(): pl.pallas_call(gather_kernel, out_shape=[jax.ShapeDtypeStruct((3, 256), F...]
where the time goes in v8:
time: 57.9 us; the launch traced here: 57.6 us
  Pallas kernels  56.8 us (98%)
  between operations  0.8 us (1%)
    pallas_call x1, Pallas kernels, gather_and_sum(): pl.pallas_call(gather_kernel, out_shape=[jax.ShapeDtypeStruct((3, 256), F...  40 us
    pallas_call x1, Pallas kernels, sweep_fields(): pl.pallas_call(sweep_kernel, out_shape=[jax.ShapeDtypeStruct((5, 16, 1638...  16.8 us

profile of v8, /device:TPU:39, one launch (start us, length us, event | category | flops | bytes accessed | tf_op | source)
XLA Modules:
  0.0 57.6 jit_solution(1877165689573389416)
XLA Ops:
  0.6 40.0 %shard_map.112 = (f32[3,256]{1,0:T(4,128)}, f32[3,256]{1,0:T(4,128)}, f32[3,16,128]{2,1,0:T(8,128)}, f32[5,3,16,128]{3,2,1,0:T(8,128)}, f32[5,8,16896]{2,1,0:T(8...) custom-call(s32[16]{0:T(128)} %counts.1, ...), custom_call_target="tpu_custom_call" | custom-call | tf_op jit(solution)/shard_map/pallas_call | solution.py:403
  40.7 16.8 %shard_map.113 = (f32[5,16,16384]{2,1,0:T(8,128)}, f32[3,256]{1,0:T(4,128)}, f32[3,256]{1,0:T(4,128)}) custom-call(f32[5,16,16384]{2,1,0:T(8,128)} %flow.3, s32[16,16384]{1,0:T(8,128)} %sections.3, f32[3,5]{1,0:T(4,128)} %viscosity.1, f32[5,8,16896]{2,1,0:T(8,128)} %get-tuple-element.13.rows_halo, f32[5,16,128]{2,1,0:T(8,128)} %get-tuple-element.14.left_halo, ...), custom_call_target="tpu_custom_call" | custom-call | tf_op jit(solution)/shard_map/pallas_call | solution.py:614
